TPU v7x, 32 devices: a whole 2x2x4 slice. The times are simulated.
32 devices in a mesh: dp: 4 (over x, core), seq: 8 (over z, y).
Axes of the slice: x: 2, y: 2, z: 4, core: 2. Of those that a mesh axis runs over, the one named last changes fastest.
Arguments:
- inputs: bfloat16 [2, 4, 1024, 1024], P(None, 'dp', 'seq'), may hold values from -6 to 6
- cotangent: bfloat16 [2, 4, 1024, 1024], P(None, 'dp', 'seq'), may hold values from -6 to 6
- segments: int32 [2, 4, 1024], P(None, 'dp'), may hold values from 0 to 5, never falling along the last dimension, each value on 1 to 768 neighbouring positions
- qkv_weight: bfloat16 [1024, 3072], P(('dp', 'seq')), may hold values from -0.1875 to 0.1875
- out_weight: bfloat16 [1024, 1024], P(('dp', 'seq')), may hold values from -0.75 to 0.75
- up_weight: bfloat16 [1024, 4096], P(('dp', 'seq')), may hold values from -0.1875 to 0.1875
- down_weight: bfloat16 [4096, 1024], P(('dp', 'seq')), may hold values from -0.09375 to 0.09375
- qv_bias: bfloat16 [2, 1024], P(None, ('dp', 'seq')), may hold values from -1.75 to 1.75
- proj_bias: bfloat16 [2, 1024], P(None, ('dp', 'seq')), may hold values from -0.625 to 0.625
- up_bias: bfloat16 [4096], P(('dp', 'seq')), may hold values from -1.75 to 1.75
- norm_gain: bfloat16 [4, 1024], P(None, ('dp', 'seq')), may hold values from 0.5 to 1.5
- norm_bias: bfloat16 [4, 1024], P(None, ('dp', 'seq')), may hold values from -1.75 to 1.75
Outputs:
- layer_out: bfloat16 [2, 4, 1024, 1024], P(None, 'dp', 'seq')
- input_grad: bfloat16 [2, 4, 1024, 1024], P(None, 'dp', 'seq')
- qkv_weight_grad: float32 [1024, 3072], P(('dp', 'seq'))
- out_weight_grad: float32 [1024, 1024], P(('dp', 'seq'))
- up_weight_grad: float32 [1024, 4096], P(('dp', 'seq'))
- down_weight_grad: float32 [4096, 1024], P(('dp', 'seq'))
- qv_bias_grad: float32 [2, 1024], P(None, ('dp', 'seq'))
- proj_bias_grad: float32 [2, 1024], P(None, ('dp', 'seq'))
- up_bias_grad: float32 [4096], P(('dp', 'seq'))
- norm_gain_grad: float32 [4, 1024], P(None, ('dp', 'seq'))
- norm_bias_grad: float32 [4, 1024], P(None, ('dp', 'seq'))
Inputs may be any that keep to these rules, and one draw needn't show every extreme that they name: `segments`: along each sequence the document numbers never fall; each of the 6 documents has 1 to 768 positions, and one has exactly 768.
All inputs are finite; a program needn't handle non-finite values.
Results may differ from a plain program's by a relative error of at most 0.012.
Values may be sent and summed in bfloat16 or wider, within the bound.
No kernel may reach another device: no remote copies, remote signals or barrier semaphores. Data moves between devices by JAX's collectives and lax.ppermute only.
A program may use at most 256 MiB of HBM per device.

v0:
```python
import jax
import jax.numpy as jnp
from jax import lax
from jax.sharding import PartitionSpec as P

D = 1024
H = 16
HD = 64
MB = 2


EPS = 1e-05
NEG = -1e30
RELAX = 32.0


def layer_norm(value, gain, shift):
    centre = jnp.mean(value, -1, keepdims=True)
    centred = value - centre
    spread = jnp.mean(centred * centred, -1, keepdims=True)
    return centred * lax.rsqrt(spread + EPS) * gain + shift


def post_attention(branch, tokens, bias, gain_one, shift_one, gain_two, shift_two):
    middle = tokens + layer_norm(branch + bias, gain_one, shift_one)
    return (middle, layer_norm(middle, gain_two, shift_two))


def activate(hidden, bias):
    return jax.nn.gelu(hidden + bias)


def finish(down, middle, bias, gain, shift):
    return middle + layer_norm(down + bias, gain, shift)


def weight_terms(active, grad_down, second, grad_hidden, attended, grad_branch, normed, grad_mixed):
    term_qkv = jnp.einsum("rd,re->de", normed, grad_mixed, preferred_element_type=jnp.float32)
    term_out = jnp.einsum("rd,re->de", attended, grad_branch, preferred_element_type=jnp.float32)
    term_up = jnp.einsum("rd,rf->df", second, grad_hidden, preferred_element_type=jnp.float32)
    term_down = jnp.einsum("rf,rd->fd", active, grad_down, preferred_element_type=jnp.float32)
    return (term_qkv, term_out, term_up, term_down)


def block_scores(query_small, keys, first, width, query_docs, key_docs, query_place):
    key_block = lax.dynamic_slice_in_dim(keys, first, width, 0)
    scores = (
        jnp.einsum("rhd,khd->hrk", query_small, key_block, preferred_element_type=jnp.float32)
        * RELAX
    )
    docs_block = lax.dynamic_slice_in_dim(key_docs, first, width, 0)
    place_block = first + jnp.arange(width, dtype=jnp.int32)
    visible = (query_place[:, None] >= place_block[None, :]) & (
        query_docs[:, None] == docs_block[None, :]
    )
    return jnp.where(visible[None], scores, NEG)


def attend_forward(query_small, keys, values, query_docs, key_docs, query_place):
    length = keys.shape[0]
    width = min(512, length)
    height = query_small.shape[0]

    def stats_step(index, carry):
        running, total = carry
        scores = block_scores(
            query_small, keys, index * width, width, query_docs, key_docs, query_place
        )
        newpeak = jnp.maximum(running, jnp.max(scores, -1))
        total = total * jnp.exp(running - newpeak) + jnp.sum(
            jnp.exp(scores - newpeak[..., None]), -1
        )
        return (newpeak, total)

    start_peak = jnp.full((H, height), NEG, jnp.float32)
    running, total = lax.fori_loop(
        0, length // width, stats_step, (start_peak, jnp.zeros((H, height), jnp.float32))
    )
    logsum = running + jnp.log(total)

    def out_step(index, summed):
        scores = block_scores(
            query_small, keys, index * width, width, query_docs, key_docs, query_place
        )
        soft = jnp.exp(scores - logsum[..., None]).astype(jnp.bfloat16)
        value_block = lax.dynamic_slice_in_dim(values, index * width, width, 0)
        return summed + jnp.einsum(
            "hrk,khd->rhd", soft, value_block, preferred_element_type=jnp.float32
        )

    attended = lax.fori_loop(0, length // width, out_step, jnp.zeros((height, H, HD), jnp.float32))
    return (attended, logsum)


def attend_backward(
    query,
    query_small,
    keys,
    values,
    grad_attended,
    logsum,
    delta,
    query_docs,
    key_docs,
    query_place,
):
    length = keys.shape[0]
    width = min(512, length)
    height = query.shape[0]

    def step(index, carry):
        grad_query, grad_keys, grad_values = carry
        first = index * width
        scores = block_scores(query_small, keys, first, width, query_docs, key_docs, query_place)
        soft = jnp.exp(scores - logsum[..., None])
        key_block = lax.dynamic_slice_in_dim(keys, first, width, 0)
        value_block = lax.dynamic_slice_in_dim(values, first, width, 0)
        grad_soft = jnp.einsum(
            "rhd,khd->hrk", grad_attended, value_block, preferred_element_type=jnp.float32
        )
        grad_scores = (soft * (grad_soft - delta[..., None])).astype(jnp.bfloat16)
        grad_query = grad_query + jnp.einsum(
            "hrk,khd->rhd", grad_scores, key_block, preferred_element_type=jnp.float32
        ) * HD ** (-0.5)
        key_part = jnp.einsum(
            "hrk,rhd->khd", grad_scores, query, preferred_element_type=jnp.float32
        ) * HD ** (-0.5)
        value_part = jnp.einsum(
            "hrk,rhd->khd",
            soft.astype(jnp.bfloat16),
            grad_attended,
            preferred_element_type=jnp.float32,
        )
        grad_keys = lax.dynamic_update_slice_in_dim(grad_keys, key_part, first, 0)
        grad_values = lax.dynamic_update_slice_in_dim(grad_values, value_part, first, 0)
        return (grad_query, grad_keys, grad_values)

    start_state = (
        jnp.zeros((height, H, HD), jnp.float32),
        jnp.zeros((length, H, HD), jnp.float32),
        jnp.zeros((length, H, HD), jnp.float32),
    )
    return lax.fori_loop(0, length // width, step, start_state)


def body(
    inputs,
    cotangent,
    segments,
    qkv_weight,
    out_weight,
    up_weight,
    down_weight,
    qv_bias,
    proj_bias,
    up_bias,
    norm_gain,
    norm_bias,
):
    height = inputs.shape[2]
    length = segments.shape[2]
    position = lax.axis_index("seq")
    query_place = position * height + jnp.arange(height, dtype=jnp.int32)
    shrink = HD ** (-0.5) / RELAX
    forward_params = (
        lax.all_gather(qkv_weight, ("dp", "seq"), axis=0, tiled=True),
        lax.all_gather(out_weight, ("dp", "seq"), axis=0, tiled=True),
        lax.all_gather(up_weight, ("dp", "seq"), axis=0, tiled=True),
        lax.all_gather(down_weight, ("dp", "seq"), axis=0, tiled=True),
        lax.all_gather(qv_bias, ("dp", "seq"), axis=1, tiled=True),
        lax.all_gather(proj_bias, ("dp", "seq"), axis=1, tiled=True),
        lax.all_gather(up_bias, ("dp", "seq"), axis=0, tiled=True),
        lax.all_gather(norm_gain, ("dp", "seq"), axis=1, tiled=True),
        lax.all_gather(norm_bias, ("dp", "seq"), axis=1, tiled=True),
    )
    w_qkv, w_out, w_up, w_down, bias_qv, bias_proj, bias_up, gains, shifts = forward_params
    gains = gains.astype(jnp.float32)
    shifts = shifts.astype(jnp.float32)
    bias_qv = bias_qv.astype(jnp.float32)
    bias_proj = bias_proj.astype(jnp.float32)
    bias_up = bias_up.astype(jnp.float32)
    results = []
    saved = []
    for batch in range(MB):
        tokens = inputs[batch, 0].astype(jnp.float32)
        key_docs = segments[batch, 0]
        query_docs = lax.dynamic_slice_in_dim(key_docs, position * height, height, 0)
        normed32, pull_first = jax.vjp(layer_norm, tokens, gains[0], shifts[0])
        normed = normed32.astype(jnp.bfloat16)
        mixed = jnp.dot(normed, w_qkv, preferred_element_type=jnp.float32)
        query = (mixed[:, :D] + bias_qv[0]).astype(jnp.bfloat16)
        keys_local = mixed[:, D : 2 * D].astype(jnp.bfloat16)
        values_local = (mixed[:, 2 * D :] + bias_qv[1]).astype(jnp.bfloat16)
        keys_all, values_all = (
            lax.all_gather(keys_local, "seq", axis=0, tiled=True),
            lax.all_gather(values_local, "seq", axis=0, tiled=True),
        )
        query_heads = query.reshape(height, H, HD)
        query_small = query_heads * shrink
        attended32, logsum = attend_forward(
            query_small,
            keys_all.reshape(length, H, HD),
            values_all.reshape(length, H, HD),
            query_docs,
            key_docs,
            query_place,
        )
        attended = attended32.reshape(height, D).astype(jnp.bfloat16)
        branch = jnp.dot(attended, w_out, preferred_element_type=jnp.float32)
        (middle, second32), pull_post = jax.vjp(
            post_attention, branch, tokens, bias_proj[0], gains[1], shifts[1], gains[2], shifts[2]
        )
        second = second32.astype(jnp.bfloat16)
        hidden = jnp.dot(second, w_up, preferred_element_type=jnp.float32)
        active32, pull_active = jax.vjp(activate, hidden, bias_up)
        active = active32.astype(jnp.bfloat16)
        down = jnp.dot(active, w_down, preferred_element_type=jnp.float32)
        result, pull_finish = jax.vjp(finish, down, middle, bias_proj[1], gains[3], shifts[3])
        results.append(result.astype(jnp.bfloat16))
        saved.append(
            (
                pull_first,
                normed,
                query,
                query_heads,
                query_small,
                keys_local,
                values_local,
                keys_all,
                values_all,
                attended,
                attended32,
                logsum,
                pull_post,
                second,
                active,
                pull_active,
                pull_finish,
                query_docs,
                key_docs,
            )
        )
    w_qkv, w_out, w_up, w_down = (
        lax.all_gather(qkv_weight, ("dp", "seq"), axis=0, tiled=True),
        lax.all_gather(out_weight, ("dp", "seq"), axis=0, tiled=True),
        lax.all_gather(up_weight, ("dp", "seq"), axis=0, tiled=True),
        lax.all_gather(down_weight, ("dp", "seq"), axis=0, tiled=True),
    )
    input_grads = []
    small_totals = None
    row_sets = []
    for batch in range(MB):
        (
            pull_first,
            normed,
            query,
            query_heads,
            query_small,
            keys_local,
            values_local,
            keys_all,
            values_all,
            attended,
            attended32,
            logsum,
            pull_post,
            second,
            active,
            pull_active,
            pull_finish,
            query_docs,
            key_docs,
        ) = saved[batch]
        grad_result = cotangent[batch, 0].astype(jnp.float32)
        grad_down32, grad_middle_a, grad_bias_down, grad_gain_three, grad_shift_three = pull_finish(
            grad_result
        )
        grad_down = grad_down32.astype(jnp.bfloat16)
        grad_active = jnp.einsum("rd,fd->rf", grad_down, w_down, preferred_element_type=jnp.float32)
        grad_hidden32, grad_bias_up = pull_active(grad_active)
        grad_hidden = grad_hidden32.astype(jnp.bfloat16)
        grad_second = jnp.einsum("rf,df->rd", grad_hidden, w_up, preferred_element_type=jnp.float32)
        (
            grad_branch32,
            grad_tokens_a,
            grad_bias_out,
            grad_gain_one,
            grad_shift_one,
            grad_gain_two,
            grad_shift_two,
        ) = pull_post((grad_middle_a, grad_second))
        grad_branch = grad_branch32.astype(jnp.bfloat16)
        grad_attended = jnp.einsum(
            "re,de->rd", grad_branch, w_out, preferred_element_type=jnp.float32
        ).astype(jnp.bfloat16)
        grad_heads = grad_attended.reshape(height, H, HD)
        delta = jnp.sum(grad_heads.astype(jnp.float32) * attended32, -1).T
        grad_query32, grad_keys_full, grad_values_full = attend_backward(
            query_heads,
            query_small,
            keys_all.reshape(length, H, HD),
            values_all.reshape(length, H, HD),
            grad_heads,
            logsum,
            delta,
            query_docs,
            key_docs,
            query_place,
        )
        grad_keys32, grad_values32 = (
            lax.psum_scatter(
                grad_keys_full.reshape(length, D).astype(jnp.bfloat16),
                "seq",
                scatter_dimension=0,
                tiled=True,
            ).astype(jnp.float32),
            lax.psum_scatter(
                grad_values_full.reshape(length, D).astype(jnp.bfloat16),
                "seq",
                scatter_dimension=0,
                tiled=True,
            ).astype(jnp.float32),
        )
        grad_query = grad_query32.reshape(height, D).astype(jnp.bfloat16)
        grad_keys = grad_keys32.astype(jnp.bfloat16)
        grad_values = grad_values32.astype(jnp.bfloat16)
        term_qv = jnp.stack(
            [
                jnp.sum(grad_query.astype(jnp.float32), 0),
                jnp.sum(grad_values.astype(jnp.float32), 0),
            ]
        )
        grad_mixed = jnp.concatenate([grad_query, grad_keys, grad_values], 1)
        grad_normed = jnp.einsum("re,de->rd", grad_mixed, w_qkv, preferred_element_type=jnp.float32)
        grad_tokens_b, grad_gain_zero, grad_shift_zero = pull_first(grad_normed)
        input_grads.append((grad_tokens_a + grad_tokens_b).astype(jnp.bfloat16))
        term_proj = jnp.stack([grad_bias_out, grad_bias_down])
        term_gain = jnp.stack([grad_gain_zero, grad_gain_one, grad_gain_two, grad_gain_three])
        term_shift = jnp.stack([grad_shift_zero, grad_shift_one, grad_shift_two, grad_shift_three])
        row_sets.append(
            (active, grad_down, second, grad_hidden, attended, grad_branch, normed, grad_mixed)
        )
        small_terms = (term_qv, term_proj, grad_bias_up, term_gain, term_shift)
        if batch == 0:
            small_totals = small_terms
        else:
            small_totals = jax.tree.map(jnp.add, small_totals, small_terms)
    joined = [jnp.concatenate([rows[k] for rows in row_sets], 0) for k in range(8)]
    term_qkv, term_out, term_up, term_down = weight_terms(
        joined[0], joined[1], joined[2], joined[3], joined[4], joined[5], joined[6], joined[7]
    )
    shards = (
        lax.psum_scatter(term_qkv, ("dp", "seq"), scatter_dimension=0, tiled=True),
        lax.psum_scatter(term_out, ("dp", "seq"), scatter_dimension=0, tiled=True),
        lax.psum_scatter(term_up, ("dp", "seq"), scatter_dimension=0, tiled=True),
        lax.psum_scatter(term_down, ("dp", "seq"), scatter_dimension=0, tiled=True),
        lax.psum_scatter(small_totals[0], ("dp", "seq"), scatter_dimension=1, tiled=True),
        lax.psum_scatter(small_totals[1], ("dp", "seq"), scatter_dimension=1, tiled=True),
        lax.psum_scatter(small_totals[2], ("dp", "seq"), scatter_dimension=0, tiled=True),
        lax.psum_scatter(small_totals[3], ("dp", "seq"), scatter_dimension=1, tiled=True),
        lax.psum_scatter(small_totals[4], ("dp", "seq"), scatter_dimension=1, tiled=True),
    )
    layer_out = jnp.stack(results)[:, None]
    input_grad = jnp.stack(input_grads)[:, None]
    return (
        layer_out,
        input_grad,
        shards[0],
        shards[1],
        shards[2],
        shards[3],
        shards[4],
        shards[5],
        shards[6],
        shards[7],
        shards[8],
    )


def solution(mesh):
    in_specs = (
        P(None, "dp", "seq", None),
        P(None, "dp", "seq", None),
        P(None, "dp", None),
        P(("dp", "seq"), None),
        P(("dp", "seq"), None),
        P(("dp", "seq"), None),
        P(("dp", "seq"), None),
        P(None, ("dp", "seq")),
        P(None, ("dp", "seq")),
        P(("dp", "seq")),
        P(None, ("dp", "seq")),
        P(None, ("dp", "seq")),
    )
    out_specs = (
        P(None, "dp", "seq", None),
        P(None, "dp", "seq", None),
        P(("dp", "seq"), None),
        P(("dp", "seq"), None),
        P(("dp", "seq"), None),
        P(("dp", "seq"), None),
        P(None, ("dp", "seq")),
        P(None, ("dp", "seq")),
        P(("dp", "seq")),
        P(None, ("dp", "seq")),
        P(None, ("dp", "seq")),
    )
    return jax.shard_map(body, mesh=mesh, in_specs=in_specs, out_specs=out_specs, check_vma=False)
```

profile of v0, /device:TPU:0, one launch (start us, length us, event | category | flops | bytes accessed | tf_op | source)
XLA Modules:
  0.0 2506.2 jit_solution(9901959166104980654)
XLA Ops:
  8.0 70.7 %all-gather = bf16[32,32,4]{1,2,0:T(4,128)(2,1)S(1)} all-gather(bf16[1,32,4]{1,2,0:T(4,128)(2,1)} %bitcast.530), channel_id=1, replica_groups=mesh['dp'=4,'seq'=8] {'dp','seq'}, dimensions={0}, use_global_device_ids=true | all-gather | bytes 8448 | tf_op jit(solution)/shard_map/all_gather | solution.py:173
  78.8 63.8 %all-gather.1 = bf16[32,32,4]{1,2,0:T(4,128)(2,1)S(1)} all-gather(bf16[1,32,4]{1,2,0:T(4,128)(2,1)} %bitcast.531), channel_id=1, replica_groups=mesh['dp'=4,'seq'=8] {'dp','seq'}, dimensions={0}, use_global_device_ids=true | all-gather | bytes 8448 | tf_op jit(solution)/shard_map/all_gather | solution.py:174
  150.9 66.0 %all-gather.2 = bf16[32,32,2]{1,2,0:T(2,128)(2,1)S(1)} all-gather(bf16[1,32,2]{1,2,0:T(2,128)(2,1)S(1)} %bitcast.532), channel_id=1, replica_groups=mesh['dp'=4,'seq'=8] {'dp','seq'}, dimensions={0}, use_global_device_ids=true | all-gather | bytes 4224 | tf_op jit(solution)/shard_map/all_gather | solution.py:170
  225.6 64.7 %all-gather.3 = bf16[32,32,2]{1,2,0:T(2,128)(2,1)S(1)} all-gather(bf16[1,32,2]{1,2,0:T(2,128)(2,1)S(1)} %bitcast.533), channel_id=1, replica_groups=mesh['dp'=4,'seq'=8] {'dp','seq'}, dimensions={0}, use_global_device_ids=true | all-gather | bytes 4224 | tf_op jit(solution)/shard_map/all_gather | solution.py:171
  290.4 66.0 %all-gather.4 = bf16[32,1,128]{2,1,0:T(2,128)(2,1)S(1)} all-gather(bf16[1,1,128]{2,1,0:T(2,128)(2,1)S(1)} %bitcast.534), channel_id=1, replica_groups=mesh['dp'=4,'seq'=8] {'dp','seq'}, dimensions={0}, use_global_device_ids=true | all-gather | bytes 8448 | tf_op jit(solution)/shard_map/all_gather | solution.py:172
  364.3 12.8 while.98
  377.1 8.1 while.99
  395.4 12.8 while.96
  408.2 8.3 while.97
  418.4 7.4 all-gather.20.cloned.1.call-done
  431.6 73.1 %all-gather.22.cloned.1.call-done = bf16[1024,4096]{1,0:T(8,128)(2,1)} async-done(((bf16[32,4096]{1,0:T(8,128)(2,1)}), bf16[1024,4096]{1,0:T(8,128)(2,1)}) %all-gather.22.cloned.1.call-update) | async-done | bytes 8388624 | tf_op jit(solution)/shard_map/all_gather | solution.py:168
  504.7 7.0 multiply_convert_fusion
  511.7 71.7 %all-gather.24.cloned.1.call-done = bf16[4096,1024]{1,0:T(8,128)(2,1)} async-done(((bf16[128,1024]{1,0:T(8,128)(2,1)}), bf16[4096,1024]{1,0:T(8,128)(2,1)}) %all-gather.24.cloned.1.call-update) | async-done | bytes 8388624 | tf_op jit(solution)/shard_map/all_gather | solution.py:169
  598.0 6.1 fusion.220
  627.3 24.3 while.100
  664.5 24.3 while.101
  705.1 17.6 reduce-scatter.39.cloned.1.call-done
  724.0 70.0 %reduce-scatter.43.cloned.1.call-done = bf16[128,1024]{1,0:T(8,128)(2,1)} async-done(((bf16[1024,1024]{1,0:T(8,128)(2,1)}), bf16[128,1024]{1,0:T(8,128)(2,1)}) %reduce-scatter.43.cloned.1.call-update) | async-done | bytes 262160
  795.3 69.7 %reduce-scatter.37.cloned.1.call-done = bf16[128,1024]{1,0:T(8,128)(2,1)} async-done(((bf16[1024,1024]{1,0:T(8,128)(2,1)}), bf16[128,1024]{1,0:T(8,128)(2,1)}) %reduce-scatter.37.cloned.1.call-update) | async-done | bytes 262160
  866.8 68.8 %reduce-scatter.41.cloned.1.call-done = bf16[128,1024]{1,0:T(8,128)(2,1)} async-done(((bf16[1024,1024]{1,0:T(8,128)(2,1)}), bf16[128,1024]{1,0:T(8,128)(2,1)}) %reduce-scatter.41.cloned.1.call-update) | async-done | bytes 262160
  954.0 6.3 fusion.114
  962.0 8.1 fusion.110
  971.7 8.1 fusion.106
  980.6 39.6 %all-reduce = f32[4096]{0:T(1024)S(1)} all-reduce(f32[4096]{0:T(1024)S(1)} %add.663), channel_id=12, replica_groups=mesh['dp'=4,'seq'=8] {'dp','seq'}, use_global_device_ids=true, to_apply=%region_70.71.clone | all-reduce | flops 4096 | bytes 32768
  1021.6 51.1 %reduce-scatter.47.cloned.1.call-done = f32[32,2]{1,0:T(8,128)} async-done(((f32[1024,2]{1,0:T(8,128)}), f32[32,2]{1,0:T(8,128)}) %reduce-scatter.47.cloned.1.call-update) | async-done | bytes 272
  1075.3 131.6 %reduce-scatter.45.cloned.1.call-done = f32[32,2]{1,0:T(8,128)} async-done(((f32[1024,2]{1,0:T(8,128)}), f32[32,2]{1,0:T(8,128)}) %reduce-scatter.45.cloned.1.call-update) | async-done | bytes 272
  1208.2 132.9 %reduce-scatter.51.cloned.1.call-done = f32[32,4]{1,0:T(8,128)} async-done(((f32[1024,4]{1,0:T(8,128)}), f32[32,4]{1,0:T(8,128)}) %reduce-scatter.51.cloned.1.call-update) | async-done | bytes 528
  1342.5 133.0 %reduce-scatter.49.cloned.1.call-done = f32[32,4]{1,0:T(8,128)} async-done(((f32[1024,4]{1,0:T(8,128)}), f32[32,4]{1,0:T(8,128)}) %reduce-scatter.49.cloned.1.call-update) | async-done | bytes 528
  1476.9 143.2 %reduce-scatter.31.cloned.1.call-done = f32[32,1024]{1,0:T(8,128)} async-done(((f32[1024,1024]{1,0:T(8,128)}), f32[32,1024]{1,0:T(8,128)}) %reduce-scatter.31.cloned.1.call-update) | async-done | bytes 131088 | tf_op jit(solution)/shard_map/reduce_scatter | solution.py:354
  1620.1 158.8 %reduce-scatter.29.cloned.1.call-done = f32[32,3072]{1,0:T(8,128)} async-done(((f32[1024,3072]{1,0:T(8,128)}), f32[32,3072]{1,0:T(8,128)}) %reduce-scatter.29.cloned.1.call-update) | async-done | bytes 393232 | tf_op jit(solution)/shard_map/reduce_scatter | solution.py:353
  1778.9 360.1 %reduce-scatter.35.cloned.1.call-done = f32[128,1024]{1,0:T(8,128)} async-done(((f32[4096,1024]{1,0:T(8,128)}), f32[128,1024]{1,0:T(8,128)}) %reduce-scatter.35.cloned.1.call-update) | async-done | bytes 524304 | tf_op jit(solution)/shard_map/reduce_scatter | solution.py:356
  2139.0 360.1 %reduce-scatter.33.cloned.1.call-done = f32[32,4096]{1,0:T(8,128)} async-done(((f32[1024,4096]{1,0:T(8,128)}), f32[32,4096]{1,0:T(8,128)}) %reduce-scatter.33.cloned.1.call-update) | async-done | bytes 524304 | tf_op jit(solution)/shard_map/reduce_scatter | solution.py:355
  (527 shorter events, 233.7 us)
Async XLA Ops:
  7.2 138.6 %copy-start.17 = (bf16[2,1,128,1024]{3,2,1,0:T(8,128)(2,1)S(1)}, bf16[2,1,128,1024]{3,2,1,0:T(8,128)(2,1)}, u32[]{:S(2)}) copy-start(bf16[2,1,128,1024]{3,2,1,0:T(8,128)(2,1)} %param.24) | copy-start | bytes 1572868
  7.2 138.9 %all-gather.14.cloned.1.call-start = ((), (), s32[]{:S(2)}) async-start(), calls=%async_computation.12 | async-start | bytes 6488064 | tf_op jit(solution)/shard_map/all_gather | solution.py:166
  7.9 349.5 %all-gather.28.cloned.1.call-start = ((), (), s32[]{:S(2)}) async-start(), calls=%async_computation.19 | async-start | bytes 2359296 | tf_op jit(solution)/shard_map/all_gather | solution.py:195
  146.0 71.0 %copy-start.41 = (bf16[128,1024]{1,0:T(8,128)(2,1)}, bf16[128,1024]{1,0:T(8,128)(2,1)S(1)}, u32[]{:S(2)}) copy-start(bf16[128,1024]{1,0:T(8,128)(2,1)S(1)} %get-tuple-element.1613) | copy-start | bytes 786436
  150.9 209.4 %all-gather.26.cloned.1.call-start = ((), (), s32[]{:S(2)}) async-start(), calls=%async_computation.18 | async-start | bytes 2359296 | tf_op jit(solution)/shard_map/all_gather | solution.py:196
  220.9 69.5 %copy-start.98 = (bf16[128]{0:T(256)(128)(2,1)S(1)}, bf16[128]{0:T(256)(128)(2,1)}, u32[]{:S(2)}) copy-start(bf16[128]{0:T(256)(128)(2,1)} %param.33) | copy-start | bytes 772
  220.9 135.5 %copy-start.91 = (s32[2,1,1024]{2,1,0:T(1,128)S(1)}, s32[2,1,1024]{2,1,0:T(1,128)}, u32[]{:S(2)}) copy-start(s32[2,1,1024]{2,1,0:T(1,128)} %param.26) | copy-start | bytes 24580
  222.0 134.5 %copy-start.73 = (bf16[128,1024]{1,0:T(8,128)(2,1)S(1)}, bf16[128,1024]{1,0:T(8,128)(2,1)}, u32[]{:S(2)}) copy-start(bf16[128,1024]{1,0:T(8,128)(2,1)} %get-tuple-element.1609) | copy-start | bytes 786436
  222.0 134.6 %copy-start.72 = (bf16[128,1024]{1,0:T(8,128)(2,1)S(1)}, bf16[128,1024]{1,0:T(8,128)(2,1)}, u32[]{:S(2)}) copy-start(bf16[128,1024]{1,0:T(8,128)(2,1)} %get-tuple-element.1643) | copy-start | bytes 786436
  222.0 165.3 %all-gather.18.cloned.1.call-start = ((), (), s32[]{:S(2)}) async-start(), calls=%async_computation.14 | async-start | bytes 2359296 | tf_op jit(solution)/shard_map/all_gather | solution.py:195
  222.8 168.5 %all-gather.16.cloned.1.call-start = ((), (), s32[]{:S(2)}) async-start(), calls=%async_computation.13 | async-start | bytes 2359296 | tf_op jit(solution)/shard_map/all_gather | solution.py:196
  223.4 202.3 %all-gather.20.cloned.1.call-start = ((), (), s32[]{:S(2)}) async-start(), calls=%async_computation.15 | async-start | bytes 2162688 | tf_op jit(solution)/shard_map/all_gather | solution.py:167
  224.0 280.7 %all-gather.22.cloned.1.call-start = ((), (), s32[]{:S(2)}) async-start(), calls=%async_computation.16 | async-start | bytes 8650752 | tf_op jit(solution)/shard_map/all_gather | solution.py:168
  224.7 358.7 %all-gather.24.cloned.1.call-start = ((), (), s32[]{:S(2)}) async-start(), calls=%async_computation.17 | async-start | bytes 8650752 | tf_op jit(solution)/shard_map/all_gather | solution.py:169
  225.5 497.3 %reduce-scatter.39.cloned.1.call-start = ((), (), s32[]{:S(2)}) async-start(), calls=%async_computation.25 | async-start | bytes 2359296
  431.6 157.2 %copy-start.65 = (bf16[128,1024]{1,0:T(8,128)(2,1)}, bf16[128,1024]{1,0:T(8,128)(2,1)S(1)}, u32[]{:S(2)}) copy-start(bf16[128,1024]{1,0:T(8,128)(2,1)S(1)} %get-tuple-element.1644) | copy-start | bytes 786436
  655.6 138.4 %reduce-scatter.43.cloned.1.call-start = ((), (), s32[]{:S(2)}) async-start(), calls=%async_computation.27 | async-start | bytes 2359296
  692.8 172.1 %reduce-scatter.37.cloned.1.call-start = ((), (), s32[]{:S(2)}) async-start(), calls=%async_computation.24 | async-start | bytes 2359296
  696.9 238.7 %reduce-scatter.41.cloned.1.call-start = ((), (), s32[]{:S(2)}) async-start(), calls=%async_computation.26 | async-start | bytes 2359296
  701.1 371.5 %reduce-scatter.47.cloned.1.call-start = ((), (), s32[]{:S(2)}) async-start(), calls=%async_computation.29 | async-start | bytes 540672
  702.3 240.5 %slice-start.2 = ((s8[6291456]{0:T(1024)(128)(4,1)}), s8[2097152]{0:T(1024)(128)(4,1)S(1)}, s32[]{:S(2)}) async-start(s8[6291456]{0:T(1024)(128)(4,1)} %bitcast.448), calls=%async_computation.34 | async-start | bytes 4194304
  705.1 501.8 %reduce-scatter.45.cloned.1.call-start = ((), (), s32[]{:S(2)}) async-start(), calls=%async_computation.28 | async-start | bytes 540672
  947.1 394.1 %reduce-scatter.51.cloned.1.call-start = ((), (), s32[]{:S(2)}) async-start(), calls=%async_computation.31 | async-start | bytes 540672
  948.2 527.3 %reduce-scatter.49.cloned.1.call-start = ((), (), s32[]{:S(2)}) async-start(), calls=%async_computation.30 | async-start | bytes 540672
  950.0 670.1 %reduce-scatter.31.cloned.1.call-start = ((), (), s32[]{:S(2)}) async-start(), calls=%async_computation.21 | async-start | bytes 4325376 | tf_op jit(solution)/shard_map/reduce_scatter | solution.py:354
  952.8 826.1 %reduce-scatter.29.cloned.1.call-start = ((), (), s32[]{:S(2)}) async-start(), calls=%async_computation.20 | async-start | bytes 12976128 | tf_op jit(solution)/shard_map/reduce_scatter | solution.py:353
  960.3 1178.6 %reduce-scatter.35.cloned.1.call-start = ((), (), s32[]{:S(2)}) async-start(), calls=%async_computation.23 | async-start | bytes 17301504 | tf_op jit(solution)/shard_map/reduce_scatter | solution.py:356
  970.1 1528.9 %reduce-scatter.33.cloned.1.call-start = ((), (), s32[]{:S(2)}) async-start(), calls=%async_computation.22 | async-start | bytes 17301504 | tf_op jit(solution)/shard_map/reduce_scatter | solution.py:355
  979.8 94.2 %copy-start.34 = (f32[128,1024]{1,0:T(8,128)S(1)}, f32[128,1024]{1,0:T(8,128)}, u32[]{:S(2)}) copy-start(f32[128,1024]{1,0:T(8,128)} %copy-done.33) | copy-start | bytes 1572868
  979.9 94.2 %copy-start.36 = (f32[128,1024]{1,0:T(8,128)S(1)}, f32[128,1024]{1,0:T(8,128)}, u32[]{:S(2)}) copy-start(f32[128,1024]{1,0:T(8,128)} %copy-done.35) | copy-start | bytes 1572868
  979.9 94.2 %copy-start.57 = (f32[128,1024]{1,0:T(8,128)S(1)}, f32[128,1024]{1,0:T(8,128)}, u32[]{:S(2)}) copy-start(f32[128,1024]{1,0:T(8,128)} %copy-done.55) | copy-start | bytes 1572868
  979.9 94.2 %copy-start.59 = (f32[128,1024]{1,0:T(8,128)S(1)}, f32[128,1024]{1,0:T(8,128)}, u32[]{:S(2)}) copy-start(f32[128,1024]{1,0:T(8,128)} %get-tuple-element.1672) | copy-start | bytes 1572868
  (109 other events, 384.6 us)
Sparse Core Ops, SparseCore 0:
  10.9 72.0 all-gather.13
  151.0 47.2 all-gather.27
  222.1 45.6 all-gather.25
  269.8 47.6 all-gather.17
  320.1 47.7 all-gather.15
  370.8 54.8 all-gather.19
  428.7 75.9 all-gather.21
  507.7 75.6 all-gather.23
  655.8 66.9 reduce-scatter.38
  726.1 67.8 reduce-scatter.42
  797.6 67.3 reduce-scatter.36
  868.3 67.1 reduce-scatter.40
  937.8 134.7 reduce-scatter.46
  1074.7 132.0 reduce-scatter.44
  1209.0 132.1 reduce-scatter.50
  1343.2 132.2 reduce-scatter.48
  1478.2 141.8 reduce-scatter.30
  1626.5 152.2 reduce-scatter.28
  1781.8 357.1 reduce-scatter.34
  2141.7 357.3 reduce-scatter.32
where the time goes:
time: 2510 us
  waiting for transfers between devices  1850 us (74%)
  blocking collectives  371 us (15%)
  matrix products  149 us (6%)
  local copies, waits for them, and re-layouts  77.7 us (3%)
  other arithmetic  37.9 us (2%)
    unnamed x28, waiting for transfers between devices  678 us
    reduce_scatter x1, waiting for transfers between devices, body(): lax.psum_scatter(term_down, ('dp', 'seq'), scatter_dimension=0, tiled=True)  360 us
    reduce_scatter x1, waiting for transfers between devices, body(): lax.psum_scatter(term_up, ('dp', 'seq'), scatter_dimension=0, tiled=True)  360 us
    reduce_scatter x1, waiting for transfers between devices, body(): lax.psum_scatter(term_qkv, ('dp', 'seq'), scatter_dimension=0, tiled=True)  159 us
    reduce_scatter x1, waiting for transfers between devices, body(): lax.psum_scatter(term_out, ('dp', 'seq'), scatter_dimension=0, tiled=True)  143 us
    all_gather x1, waiting for transfers between devices, body(): lax.all_gather(up_weight, ('dp', 'seq'), axis=0, tiled=True)  73.1 us
    all_gather x1, waiting for transfers between devices, body(): lax.all_gather(down_weight, ('dp', 'seq'), axis=0, tiled=True)  71.7 us
    all_gather x1, blocking collectives, body(): lax.all_gather(norm_gain, ('dp', 'seq'), axis=1, tiled=True)  70.7 us
  transfers between devices with their start and end apart: 20, of which 15 were waited for; matrix products, arithmetic and copies ran while one was open for 7% of the time, Pallas kernels for 0%

commit v1 on v0

v1 whole, which is shorter than its diff:
```python
import functools

import jax
import jax.numpy as jnp
from jax import lax
from jax.experimental import pallas as pl
from jax.experimental.pallas import tpu as pltpu
from jax.sharding import PartitionSpec as P

D = 1024
H = 16
HD = 64
MB = 2

EPS = 1e-05
NEG = -1e30
SHRINK = HD ** (-0.5)
BF16 = jnp.bfloat16
F32 = jnp.float32
C0 = 0.7978845608028654
C1 = 0.044715


def dot(a, b, dims):
    return lax.dot_general(a, b, (dims, ((), ())), preferred_element_type=F32)


def head_mask(x, h, heads):
    if heads == 1:
        return x
    lane = lax.broadcasted_iota(jnp.int32, x.shape, 1)
    return jnp.where(lane // HD == h, x, jnp.zeros_like(x))


def transpose(x):
    return x.astype(F32).T


def attend_forward_kernel(
    heads, blk, pos_ref, lo_ref, start_ref, q_ref, k_ref, v_ref, o_ref, ot_ref, lse_ref, qn, kn, vt
):
    slots, rows = q_ref.shape[0], q_ref.shape[2]
    length = qn.shape[0]
    batch = pl.program_id(0)
    for j in range(slots):
        at = pl.multiple_of(pos_ref[j] * rows, rows)
        qn[pl.ds(at, rows), :] = q_ref[j, 0]
        kn[pl.ds(at, rows), :] = k_ref[j, 0]
        vt[:, pl.ds(at, rows)] = transpose(v_ref[j, 0]).astype(BF16)
    for i in range(length // blk):
        start = start_ref[0, 0:1, i * blk : (i + 1) * blk]
        qpos = i * blk + lax.broadcasted_iota(jnp.int32, (blk, blk), 1)
        base = lax.broadcasted_iota(jnp.int32, (blk, blk), 0)
        for h in range(heads):
            qh = head_mask(qn[i * blk : (i + 1) * blk, :], h, heads) * BF16(SHRINK)

            def step(j, carry, qh=qh, start=start, qpos=qpos, base=base, h=h):
                peak, total, acc = carry
                first = pl.multiple_of(j * blk, blk)
                st = dot(kn[pl.ds(first, blk), :], qh, ((1,), (1,)))
                kpos = base + first
                st = jnp.where((kpos >= start) & (kpos <= qpos), st, NEG)
                new = jnp.maximum(peak, jnp.max(st, 0, keepdims=True))
                pt = jnp.exp(st - new)
                keep = jnp.exp(peak - new)
                total = total * keep + jnp.sum(pt, 0, keepdims=True)
                vh = vt[h * HD : (h + 1) * HD, pl.ds(first, blk)]
                acc = acc * keep + dot(vh, pt.astype(BF16), ((1,), (0,)))
                return (new, total, acc)

            init = (
                jnp.full((1, blk), NEG, F32),
                jnp.zeros((1, blk), F32),
                jnp.zeros((HD, blk), F32),
            )
            peak, total, acc = lax.fori_loop(lo_ref[batch, i], i + 1, step, init)
            lse_ref[0, h : h + 1, i * blk : (i + 1) * blk] = peak + jnp.log(total)
            ot_ref[0, h * HD : (h + 1) * HD, i * blk : (i + 1) * blk] = acc / total
    for j in range(slots):
        o_ref[j, 0] = ot_ref[0, :, j * rows : (j + 1) * rows].T.astype(BF16)


def attend_backward_kernel(
    heads,
    blk,
    pos_ref,
    hi_ref,
    start_ref,
    q_ref,
    k_ref,
    v_ref,
    ga_ref,
    ot_ref,
    lse_ref,
    dq_ref,
    dk_ref,
    dv_ref,
    qn,
    kn,
    vn,
    gan,
    kt,
    dqt,
    dkn,
    dvn,
    delta,
):
    slots, rows = q_ref.shape[0], q_ref.shape[2]
    length = qn.shape[0]
    batch = pl.program_id(0)
    for j in range(slots):
        at = pl.multiple_of(pos_ref[j] * rows, rows)
        qn[pl.ds(at, rows), :] = q_ref[j, 0] * BF16(SHRINK)
        kn[pl.ds(at, rows), :] = k_ref[j, 0]
        vn[pl.ds(at, rows), :] = v_ref[j, 0]
        kt[:, pl.ds(at, rows)] = transpose(k_ref[j, 0]).astype(BF16)
        ga = ga_ref[j, 0]
        gan[j * rows : (j + 1) * rows, :] = ga
        prod = transpose(ga) * ot_ref[0, :, j * rows : (j + 1) * rows]
        for h in range(heads):
            delta[h : h + 1, j * rows : (j + 1) * rows] = jnp.sum(
                prod[h * HD : (h + 1) * HD], 0, keepdims=True
            )
    dqt[...] = jnp.zeros_like(dqt)
    for j in range(length // blk):
        key = kn[j * blk : (j + 1) * blk, :]
        value = vn[j * blk : (j + 1) * blk, :]
        kpos = j * blk + lax.broadcasted_iota(jnp.int32, (blk, blk), 0)
        base = lax.broadcasted_iota(jnp.int32, (blk, blk), 1)

        def step(i, carry, key=key, value=value, kpos=kpos, base=base, j=j):
            dk, dv = carry
            first = pl.multiple_of(i * blk, blk)
            cols = pl.ds(first, blk)
            start = start_ref[0, 0:1, cols]
            visible = (kpos >= start) & (kpos <= base + first)
            qall = qn[cols, :]
            gall = gan[cols, :]
            for h in range(heads):
                qh = head_mask(qall, h, heads)
                gh = head_mask(gall, h, heads)
                st = dot(key, qh, ((1,), (1,)))
                pt = jnp.where(visible, jnp.exp(st - lse_ref[0, h : h + 1, cols]), 0.0)
                dpt = dot(value, gh, ((1,), (1,)))
                dst = (pt * (dpt - delta[h : h + 1, cols])).astype(BF16)
                dv = dv + dot(pt.astype(BF16), gh, ((1,), (0,)))
                dk = dk + dot(dst, qh, ((1,), (0,)))
                part = dot(kt[h * HD : (h + 1) * HD, j * blk : (j + 1) * blk], dst, ((1,), (0,)))
                dqt[h * HD : (h + 1) * HD, cols] = dqt[h * HD : (h + 1) * HD, cols] + part
            return (dk, dv)

        zero = jnp.zeros((blk, heads * HD), F32)
        dk, dv = lax.fori_loop(j, hi_ref[batch, j] + 1, step, (zero, zero))
        dkn[j * blk : (j + 1) * blk, :] = dk.astype(BF16)
        dvn[j * blk : (j + 1) * blk, :] = dv.astype(BF16)
    for j in range(slots):
        at = pl.multiple_of(pos_ref[j] * rows, rows)
        dq_ref[j, 0] = ((dqt[:, pl.ds(at, rows)] * SHRINK).T).astype(BF16)
        dk_ref[j, 0] = dkn[pl.ds(at, rows), :]
        dv_ref[j, 0] = dvn[pl.ds(at, rows), :]


def attention_specs(slots, rows, lanes, length, heads):
    piece = pl.BlockSpec((slots, 1, rows, lanes), lambda b, *_: (0, b, 0, 0))
    starts = pl.BlockSpec((1, 1, length), lambda b, *_: (b, 0, 0))
    turned = pl.BlockSpec((1, lanes, length), lambda b, *_: (b, 0, 0))
    sums = pl.BlockSpec((1, heads, length), lambda b, *_: (b, 0, 0))
    return piece, starts, turned, sums


def attend_forward(pos, lo, start, q, k, v, blk):
    slots, batches, rows, lanes = q.shape
    length, heads = slots * rows, lanes // HD
    piece, starts, turned, sums = attention_specs(slots, rows, lanes, length, heads)
    pairs = batches * heads * length * length
    return pl.pallas_call(
        functools.partial(attend_forward_kernel, heads, blk),
        out_shape=(
            jax.ShapeDtypeStruct(q.shape, BF16),
            jax.ShapeDtypeStruct((batches, lanes, length), F32),
            jax.ShapeDtypeStruct((batches, heads, length), F32),
        ),
        grid_spec=pltpu.PrefetchScalarGridSpec(
            num_scalar_prefetch=2,
            grid=(batches,),
            in_specs=[starts, piece, piece, piece],
            out_specs=[piece, turned, sums],
            scratch_shapes=[
                pltpu.VMEM((length, lanes), BF16),
                pltpu.VMEM((length, lanes), BF16),
                pltpu.VMEM((lanes, length), BF16),
            ],
        ),
        cost_estimate=pl.CostEstimate(
            flops=pairs * 4 * HD, bytes_accessed=q.size * 16, transcendentals=pairs
        ),
        name="attend_forward",
    )(pos, lo, start, q, k, v)


def attend_backward(pos, hi, start, q, k, v, ga, ot, lse, blk):
    slots, batches, rows, lanes = q.shape
    length, heads = slots * rows, lanes // HD
    piece, starts, turned, sums = attention_specs(slots, rows, lanes, length, heads)
    pairs = batches * heads * length * length
    return pl.pallas_call(
        functools.partial(attend_backward_kernel, heads, blk),
        out_shape=(jax.ShapeDtypeStruct(q.shape, BF16),) * 3,
        grid_spec=pltpu.PrefetchScalarGridSpec(
            num_scalar_prefetch=2,
            grid=(batches,),
            in_specs=[starts, piece, piece, piece, piece, turned, sums],
            out_specs=[piece, piece, piece],
            scratch_shapes=[pltpu.VMEM((length, lanes), BF16)] * 4
            + [
                pltpu.VMEM((lanes, length), BF16),
                pltpu.VMEM((lanes, length), F32),
                pltpu.VMEM((length, lanes), BF16),
                pltpu.VMEM((length, lanes), BF16),
                pltpu.VMEM((heads, length), F32),
            ],
        ),
        cost_estimate=pl.CostEstimate(
            flops=pairs * 10 * HD, bytes_accessed=q.size * 20, transcendentals=pairs
        ),
        name="attend_backward",
    )(pos, hi, start, q, k, v, ga, ot, lse)


def gelu_parts(h):
    t = jnp.tanh(C0 * (h + C1 * (h * h * h)))
    return t, 0.5 * h * (1.0 + t)


def gelu_slope(h):
    t = jnp.tanh(C0 * (h + C1 * (h * h * h)))
    return 0.5 * (1.0 + t) + 0.5 * h * (1.0 - t * t) * (C0 * (1.0 + 3.0 * C1 * (h * h)))


def gelu_forward_kernel(order_ref, h_ref, a_ref):
    width = 128

    def step(j, carry):
        src = pl.multiple_of(order_ref[j] * width, width)
        dst = pl.multiple_of(j * width, width)
        a_ref[:, pl.ds(dst, width)] = gelu_parts(h_ref[:, pl.ds(src, width)])[1].astype(BF16)
        return carry

    lax.fori_loop(0, h_ref.shape[1] // width, step, 0)


def gelu_backward_kernel(order_ref, h_ref, ga_ref, gh_ref, sum_ref):
    width = 128

    @pl.when(pl.program_id(0) == 0)
    def _():
        sum_ref[...] = jnp.zeros_like(sum_ref)

    def step(j, carry):
        dst = pl.multiple_of(order_ref[j] * width, width)
        src = pl.multiple_of(j * width, width)
        g = ga_ref[:, pl.ds(src, width)] * gelu_slope(h_ref[:, pl.ds(dst, width)])
        gh_ref[:, pl.ds(dst, width)] = g.astype(BF16)
        sum_ref[:, pl.ds(dst, width)] = sum_ref[:, pl.ds(dst, width)] + jnp.sum(
            g, 0, keepdims=True
        )
        return carry

    lax.fori_loop(0, h_ref.shape[1] // width, step, 0)


def chunk_order(order, height):
    many = height // 128
    return (order[:, None] * many + jnp.arange(many, dtype=jnp.int32)[None]).reshape(-1)


def gelu_forward(hidden, order, height):
    rows, width = hidden.shape
    if height % 128:
        act = gelu_parts(hidden)[1].astype(BF16).reshape(rows, -1, height)
        return jnp.take(act, order, axis=1).reshape(rows, width)
    tall = min(rows, 64)
    spec = pl.BlockSpec((tall, width), lambda i, *_: (i, 0))
    return pl.pallas_call(
        gelu_forward_kernel,
        out_shape=jax.ShapeDtypeStruct((rows, width), BF16),
        grid_spec=pltpu.PrefetchScalarGridSpec(
            num_scalar_prefetch=1, grid=(rows // tall,), in_specs=[spec], out_specs=spec
        ),
        cost_estimate=pl.CostEstimate(
            flops=rows * width * 10, bytes_accessed=rows * width * 6, transcendentals=rows * width
        ),
        name="gelu_forward",
    )(chunk_order(order, height), hidden)


def gelu_backward(hidden, grad, order, height):
    rows, width = hidden.shape
    if height % 128:
        back = jnp.argsort(order)
        grad = jnp.take(grad.reshape(rows, -1, height), back, axis=1).reshape(rows, width)
        grad = grad * gelu_slope(hidden)
        return grad.astype(BF16), jnp.sum(grad, 0, keepdims=True)
    tall = min(rows, 64)
    spec = pl.BlockSpec((tall, width), lambda i, *_: (i, 0))
    return pl.pallas_call(
        gelu_backward_kernel,
        out_shape=(
            jax.ShapeDtypeStruct((rows, width), BF16),
            jax.ShapeDtypeStruct((1, width), F32),
        ),
        grid_spec=pltpu.PrefetchScalarGridSpec(
            num_scalar_prefetch=1,
            grid=(rows // tall,),
            in_specs=[spec, spec],
            out_specs=[spec, pl.BlockSpec((1, width), lambda i, *_: (0, 0))],
        ),
        cost_estimate=pl.CostEstimate(
            flops=rows * width * 20, bytes_accessed=rows * width * 10, transcendentals=rows * width
        ),
        name="gelu_backward",
    )(chunk_order(order, height), hidden, grad)


class Net:
    def __init__(self, n_dp, n_seq):
        self.n_dp, self.n_seq = n_dp, n_seq
        self.nx, self.nz = n_dp // 2, n_seq // 2
        self.core = [(i, i ^ 1) for i in range(n_dp)]
        self.y = [(i, i ^ 1) for i in range(n_seq)]
        self.x_next = [(i, (i + 2) % n_dp) for i in range(n_dp)]
        self.z_next = [(i, (i + 2) % n_seq) for i in range(n_seq)]
        self.x_prev = [(b, a) for a, b in self.x_next]
        self.z_prev = [(b, a) for a, b in self.z_next]
        self.d = lax.axis_index("dp")
        self.s = lax.axis_index("seq")

    def seq_order(self):
        k = jnp.arange(self.nz, dtype=jnp.int32)[:, None]
        yr = jnp.arange(2, dtype=jnp.int32)[None, :]
        z = lax.rem(self.s // 2 - k + self.nz, self.nz)
        return (z * 2 + jnp.bitwise_xor(lax.rem(self.s, 2), yr)).reshape(-1).astype(jnp.int32)

    def all_order(self):
        j = jnp.arange(self.nx, dtype=jnp.int32)[None, :]
        c = jnp.arange(2, dtype=jnp.int32)[:, None]
        x = lax.rem(self.d // 2 - j + self.nx, self.nx)
        dp = x * 2 + jnp.bitwise_xor(lax.rem(self.d, 2), c)
        seq = self.seq_order().reshape(self.nz, 2)
        return (dp[None, :, :, None] * self.n_seq + seq[:, None, None, :]).reshape(-1)

    def gather_seq(self, a):
        ring = [a]
        for _ in range(self.nz - 1):
            ring.append(lax.ppermute(ring[-1], "seq", self.z_next))
        slots = []
        for piece in ring:
            slots += [piece, lax.ppermute(piece, "seq", self.y)]
        return slots

    def gather_all(self, a):
        pieces = []
        slots = self.gather_seq(a)
        for k in range(self.nz):
            pair = jnp.concatenate(slots[2 * k : 2 * k + 2], 0)
            ring = [pair]
            for _ in range(self.nx - 1):
                ring.append(lax.ppermute(ring[-1], "dp", self.x_next))
            quad = jnp.concatenate(ring, 0)
            pieces += [quad, lax.ppermute(quad, "dp", self.core)]
        return pieces

    def scatter_all(self, left, right):
        step = left.shape[1] // (2 * self.nz)
        height = step // (2 * self.nx)
        done = None
        for k in reversed(range(self.nz)):
            at = 2 * k * step
            away = dot(left[:, at + step : at + 2 * step], right, ((0,), (0,))).astype(BF16)
            own = dot(left[:, at : at + step], right, ((0,), (0,)))
            own = own + lax.ppermute(away, "dp", self.core).astype(F32)
            own = own.reshape(self.nx, 2 * height, -1)
            total = own[self.nx - 1]
            for j in reversed(range(self.nx - 1)):
                total = own[j] + lax.ppermute(total.astype(BF16), "dp", self.x_prev).astype(F32)
            total = total[:height] + lax.ppermute(
                total[height:].astype(BF16), "seq", self.y
            ).astype(F32)
            if done is not None:
                total = total + lax.ppermute(done.astype(BF16), "seq", self.z_prev).astype(F32)
            done = total
        return done

    def scatter_seq(self, slots):
        done = None
        for k in reversed(range(self.nz)):
            total = slots[2 * k] + lax.ppermute(
                slots[2 * k + 1].astype(BF16), "seq", self.y
            ).astype(F32)
            if done is not None:
                total = total + lax.ppermute(done.astype(BF16), "seq", self.z_prev).astype(F32)
            done = total
        return done

    def gather_small(self, a):
        n_dp, n_seq = self.n_dp, self.n_seq
        rows = [a]
        for t in range(1, n_seq):
            rows.append(lax.ppermute(a, "seq", [(i, (i + t) % n_seq) for i in range(n_seq)]))
        group = jnp.stack(rows)
        groups = [group]
        for u in range(1, n_dp):
            groups.append(lax.ppermute(group, "dp", [(i, (i + u) % n_dp) for i in range(n_dp)]))
        mixed = jnp.concatenate(groups, 0)
        u = jnp.arange(n_dp, dtype=jnp.int32)[:, None]
        t = jnp.arange(n_seq, dtype=jnp.int32)[None, :]
        order = lax.rem(self.d - u + n_dp, n_dp) * n_seq + lax.rem(self.s - t + n_seq, n_seq)
        place = jnp.arange(n_dp * n_seq, dtype=jnp.int32)[:, None] == order.reshape(1, -1)
        return dot(place.astype(BF16), mixed, ((1,), (0,)))


def swap_all(a, axis_name):
    return lax.all_to_all(a, axis_name, 0, 0, tiled=True)


def ln_stats(value):
    centre = jnp.mean(value, -1, keepdims=True)
    centred = value - centre
    spread = jnp.mean(centred * centred, -1, keepdims=True)
    root = lax.rsqrt(spread + EPS)
    return centred * root, root


def ln_back(unit, root, gain, grad):
    c = grad * gain
    return root * (
        c
        - jnp.mean(c, -1, keepdims=True)
        - unit * jnp.mean(c * unit, -1, keepdims=True)
    )


def body(
    n_dp,
    n_seq,
    inputs,
    cotangent,
    segments,
    qkv_weight,
    out_weight,
    up_weight,
    down_weight,
    qv_bias,
    proj_bias,
    up_bias,
    norm_gain,
    norm_bias,
):
    net = Net(n_dp, n_seq)
    devices = n_dp * n_seq
    height = inputs.shape[2]
    length = segments.shape[2]
    count = MB * height
    heads = H // n_seq
    lanes = heads * HD
    blk = min(256, length)
    order = net.all_order()
    pos = net.seq_order()
    tokens16 = inputs.reshape(count, D)
    tokens = tokens16.astype(F32)

    token_slots = net.gather_seq(tokens16)
    small = jnp.concatenate(
        [a.reshape(-1) for a in (qv_bias, proj_bias, up_bias, norm_gain, norm_bias)]
    )
    small = net.gather_small(small)
    share = D // devices
    wide = up_bias.shape[0]

    def unpack(first, many):
        part = small[:, first : first + many * share].reshape(devices, many, share)
        return part.transpose(1, 0, 2).reshape(many, D)

    bias_qv = unpack(0, 2)
    bias_proj = unpack(2 * share, 2)
    bias_up = small[:, 4 * share : 4 * share + wide].reshape(1, devices * wide)
    gains = unpack(4 * share + wide, 4)
    shifts = unpack(8 * share + wide, 4)

    rows_out, rows_qkv = out_weight.shape[0], qkv_weight.shape[0]
    mine = qkv_weight.reshape(rows_qkv, 3, n_seq, lanes).transpose(2, 0, 1, 3)
    mine = swap_all(mine.reshape(n_seq, rows_qkv, 3 * lanes), "seq")
    mine = mine.reshape(n_seq * rows_qkv, 3 * lanes)
    w_heads = jnp.zeros((D, 3 * lanes), BF16)
    for u in range(n_dp):
        part = mine
        if u:
            part = lax.ppermute(mine, "dp", [(i, (i + u) % n_dp) for i in range(n_dp)])
        at = lax.rem(net.d - u + n_dp, n_dp) * (n_seq * rows_qkv)
        w_heads = lax.dynamic_update_slice(w_heads, part, (at, jnp.int32(0)))

    first_pieces = net.gather_all(jnp.concatenate([out_weight, up_weight], 1))
    w_out = jnp.concatenate([p[:, :D] for p in first_pieces], 0)
    w_up = jnp.concatenate([p[:, D:] for p in first_pieces], 0)
    w_down = jnp.concatenate(net.gather_all(down_weight), 0)

    source = (order[:, None] * rows_out + jnp.arange(rows_out, dtype=jnp.int32)[None]).reshape(1, D)
    shuffle = (jnp.arange(D, dtype=jnp.int32)[:, None] == source).astype(BF16)

    docs = segments[:, 0]
    start = jnp.sum((docs[:, None, :] < docs[:, :, None]).astype(jnp.int32), -1)
    low = start[:, ::blk] // blk
    last = docs[:, blk - 1 :: blk]
    high = (jnp.sum((docs[:, None, :] <= last[:, :, None]).astype(jnp.int32), -1) - 1) // blk
    start = start[:, None, :]

    at = net.s * lanes
    bias_q = lax.dynamic_slice(bias_qv, (jnp.int32(0), at), (1, lanes))
    bias_v = lax.dynamic_slice(bias_qv, (jnp.int32(1), at), (1, lanes))
    bias_heads = jnp.concatenate([bias_q, jnp.zeros_like(bias_q), bias_v], 1)
    normed, mixed, units = [], [], []
    for piece in token_slots:
        unit, _ = ln_stats(piece.astype(F32))
        line = (unit * gains[0] + shifts[0]).astype(BF16)
        normed.append(line)
        units.append(unit)
        mixed.append((dot(line, w_heads, ((1,), (0,))) + bias_heads).astype(BF16))

    def part_of(k):
        parts = [m[:, k * lanes : (k + 1) * lanes] for m in mixed]
        return jnp.stack(parts).reshape(n_seq, MB, height, lanes)

    query, keys, values = part_of(0), part_of(1), part_of(2)
    attended_heads, turned, logsum = attend_forward(pos, low, start, query, keys, values, blk)
    attended = swap_all(attended_heads, "seq").reshape(n_seq, count, lanes)
    attended = attended.transpose(1, 0, 2).reshape(count, D)
    attended = dot(attended, shuffle, ((1,), (0,))).astype(BF16)

    branch = dot(attended, w_out, ((1,), (0,))) + bias_proj[0]
    unit_one, root_one = ln_stats(branch)
    middle = tokens + (unit_one * gains[1] + shifts[1])
    unit_two, root_two = ln_stats(middle)
    second = (unit_two * gains[2] + shifts[2]).astype(BF16)
    second = dot(second, shuffle, ((1,), (0,))).astype(BF16)
    hidden = dot(second, w_up, ((1,), (0,))) + bias_up
    active = gelu_forward(hidden, order, down_weight.shape[0])
    down = dot(active, w_down, ((1,), (0,))) + bias_proj[1]
    unit_three, root_three = ln_stats(down)
    layer_out = (middle + (unit_three * gains[3] + shifts[3])).astype(BF16)

    dy = cotangent.reshape(count, D).astype(F32)
    grad_gain_three = jnp.sum(dy * unit_three, 0)
    grad_shift_three = jnp.sum(dy, 0)
    grad_down32 = ln_back(unit_three, root_three, gains[3], dy)
    grad_bias_down = jnp.sum(grad_down32, 0)
    grad_down = grad_down32.astype(BF16)
    grad_active = dot(grad_down, w_down, ((1,), (1,)))
    shard_down = net.scatter_all(active, grad_down)
    grad_hidden, grad_bias_up = gelu_backward(hidden, grad_active, order, down_weight.shape[0])
    grad_second = dot(grad_hidden, w_up, ((1,), (1,)))
    shard_up = net.scatter_all(second, grad_hidden)
    upper = grad_second.astype(BF16)
    lower = (grad_second - upper.astype(F32)).astype(BF16)
    grad_second = dot(upper, shuffle, ((1,), (1,))) + dot(lower, shuffle, ((1,), (1,)))
    grad_gain_two = jnp.sum(grad_second * unit_two, 0)
    grad_shift_two = jnp.sum(grad_second, 0)
    grad_middle = dy + ln_back(unit_two, root_two, gains[2], grad_second)
    grad_gain_one = jnp.sum(grad_middle * unit_one, 0)
    grad_shift_one = jnp.sum(grad_middle, 0)
    grad_branch32 = ln_back(unit_one, root_one, gains[1], grad_middle)
    grad_bias_out = jnp.sum(grad_branch32, 0)
    grad_branch = grad_branch32.astype(BF16)
    grad_attended = dot(grad_branch, w_out, ((1,), (1,))).astype(BF16)
    shard_out = net.scatter_all(attended, grad_branch)
    grad_attended = dot(grad_attended, shuffle, ((1,), (1,))).astype(BF16)
    grad_attended = grad_attended.reshape(count, n_seq, lanes).transpose(1, 0, 2)
    grad_heads = swap_all(grad_attended, "seq").reshape(n_seq, MB, height, lanes)
    dq, dk, dv = attend_backward(
        pos, high, start, query, keys, values, grad_heads, turned, logsum, blk
    )
    grad_mixed = jnp.concatenate([dq, dk, dv], -1).reshape(n_seq * count, 3 * lanes)
    grad_bias_heads = jnp.sum(grad_mixed.astype(F32), 0)
    grad_normed = dot(grad_mixed, w_heads, ((1,), (1,))).reshape(n_seq, count, D)
    back = net.scatter_seq([grad_normed[j] for j in range(n_seq)])
    grad_gain_zero = sum(jnp.sum(grad_normed[j] * units[j], 0) for j in range(n_seq))
    grad_shift_zero = jnp.sum(grad_normed, (0, 1))
    unit_zero, root_zero = ln_stats(tokens)
    input_grad = (grad_middle + ln_back(unit_zero, root_zero, gains[0], back)).astype(BF16)

    term = dot(jnp.concatenate(normed, 0), grad_mixed, ((0,), (0,))).astype(BF16)
    term = swap_all(term.reshape(n_dp, n_seq * rows_qkv, 3 * lanes), "dp")
    term = jnp.sum(term.astype(F32), 0).astype(BF16)
    term = swap_all(term.reshape(n_seq, rows_qkv, 3 * lanes), "seq")
    term = term.reshape(n_seq, rows_qkv, 3, lanes).transpose(1, 2, 0, 3)
    shard_qkv = term.reshape(rows_qkv, 3 * D).astype(F32)

    def pack(vectors):
        many = len(vectors)
        return jnp.stack(vectors).reshape(many, devices, share).transpose(1, 0, 2).reshape(
            devices, many * share
        )

    grad_q = lax.dynamic_update_slice(jnp.zeros((D,), F32), grad_bias_heads[:lanes], (at,))
    grad_v = lax.dynamic_update_slice(jnp.zeros((D,), F32), grad_bias_heads[2 * lanes :], (at,))
    sums = jnp.concatenate(
        [
            pack([grad_q, grad_v, grad_bias_out, grad_bias_down]),
            grad_bias_up.reshape(devices, wide),
            pack([grad_gain_zero, grad_gain_one, grad_gain_two, grad_gain_three]),
            pack([grad_shift_zero, grad_shift_one, grad_shift_two, grad_shift_three]),
        ],
        1,
    )
    each = sums.shape[1]
    sums = sums.reshape(n_dp, n_seq, each).transpose(1, 0, 2).reshape(n_seq, n_dp * each)
    sums = jnp.sum(swap_all(sums, "seq"), 0).reshape(n_dp, each)
    sums = jnp.sum(swap_all(sums, "dp"), 0)
    first = 4 * share + wide

    return (
        layer_out.reshape(MB, 1, height, D),
        input_grad.reshape(MB, 1, height, D),
        shard_qkv,
        shard_out,
        shard_up,
        shard_down,
        sums[: 2 * share].reshape(2, share),
        sums[2 * share : 4 * share].reshape(2, share),
        sums[4 * share : first],
        sums[first : first + 4 * share].reshape(4, share),
        sums[first + 4 * share :].reshape(4, share),
    )


def solution(mesh):
    both = ("dp", "seq")
    in_specs = (
        P(None, "dp", "seq", None),
        P(None, "dp", "seq", None),
        P(None, "dp", None),
        P(both, None),
        P(both, None),
        P(both, None),
        P(both, None),
        P(None, both),
        P(None, both),
        P(both),
        P(None, both),
        P(None, both),
    )
    out_specs = (
        P(None, "dp", "seq", None),
        P(None, "dp", "seq", None),
        P(both, None),
        P(both, None),
        P(both, None),
        P(both, None),
        P(None, both),
        P(None, both),
        P(both),
        P(None, both),
        P(None, both),
    )
    step = functools.partial(body, mesh.shape["dp"], mesh.shape["seq"])
    return jax.shard_map(step, mesh=mesh, in_specs=in_specs, out_specs=out_specs, check_vma=False)
```

time: 2510 us -> 697 us (0.28)
  waiting for transfers between devices: 1850 us -> 216 us
  blocking collectives: 371 us -> 0 us
  starting transfers between devices: 1.07 us -> 154 us
  matrix products: 149 us -> 90 us
  Pallas kernels: 0 us -> 53.1 us
  other arithmetic: 37.9 us -> 65.4 us
  local copies, waits for them, and re-layouts: 77.7 us -> 105 us
    reduce_scatter x4 -> x0, waiting for transfers between devices: 1020 us -> none  [the longest x1 360 us: body(): lax.psum_scatter(term_down, ('dp', 'seq'), scatter_dimension=0, tiled=True)]
    unnamed x28 -> x0, waiting for transfers between devices: 678 us -> none
    all_gather x5 -> x0, blocking collectives: 331 us -> none  [the longest x1 70.7 us: body(): lax.all_gather(norm_gain, ('dp', 'seq'), axis=1, tiled=True)]
    ppermute x0 -> x102, waiting for transfers between devices: none -> 214 us  [the longest x12 56.9 us: gather_seq(): slots += [piece, lax.ppermute(piece, 'seq', self.y)]]
    all_gather x8 -> x0, waiting for transfers between devices: 152 us -> none  [the longest x1 73.1 us: body(): lax.all_gather(up_weight, ('dp', 'seq'), axis=0, tiled=True)]
    ppermute x0 -> x102, starting transfers between devices: none -> 124 us  [the longest x9 21.6 us: scatter_all(): lax.ppermute(done.astype(BF16), 'seq', self.z_prev).astype(F32)]
    dot_general x48 -> x45, matrix products: 149 us -> 90 us  [dot(): return lax.dot_general(a, b, (dims, ((), ())), preferred_element_type=F32)]
    pallas_call x0 -> x4, Pallas kernels: none -> 53.1 us  [the longest x1 20.5 us: attend_forward(): pl.pallas_call(functools.partial(attend_forward_kernel, heads, blk), out_...]
  transfers between devices with their start and end apart: 20 -> 109, of which waited for: 15 -> 35; matrix products, arithmetic and copies ran while one was open for 7% -> 27% of each run, Pallas kernels for 0% -> 6%
where the time goes in v1:
time: 697 us; the launch traced here: 687 us
  waiting for transfers between devices  216 us (31%)
  starting transfers between devices  154 us (22%)
  local copies, waits for them, and re-layouts  105 us (15%)
  matrix products  90 us (13%)
  other arithmetic  65.4 us (9%)
  Pallas kernels  53.1 us (8%)
    dot_general x45, matrix products, dot(): return lax.dot_general(a, b, (dims, ((), ())), preferred_element_type=F32)  90 us
    unnamed x326, local copies, waits for them, and re-layouts  59.5 us
    ppermute x12, waiting for transfers between devices, gather_seq(): slots += [piece, lax.ppermute(piece, 'seq', self.y)]  56.9 us
    ppermute x12, waiting for transfers between devices, scatter_all(): lax.ppermute(total.astype(BF16), 'dp', self.x_prev).astype(F32)  54.1 us
    all_to_all x7, starting transfers between devices, swap_all(): return lax.all_to_all(a, axis_name, 0, 0, tiled=True)  30.2 us
    ppermute x8, waiting for transfers between devices, gather_all(): ring.append(lax.ppermute(ring[-1], 'dp', self.x_next))  28.9 us
    ppermute x9, waiting for transfers between devices, gather_seq(): ring.append(lax.ppermute(ring[-1], 'seq', self.z_next))  27.8 us
    ppermute x9, starting transfers between devices, scatter_all(): lax.ppermute(done.astype(BF16), 'seq', self.z_prev).astype(F32)  21.6 us
  transfers between devices with their start and end apart: 109, of which 35 were waited for; matrix products, arithmetic and copies ran while one was open for 27% of the time, Pallas kernels for 6%

profile of v1, /device:TPU:0, one launch (start us, length us, event | category | flops | bytes accessed | tf_op | source)
XLA Modules:
  0.0 686.9 jit_solution(13819030710829468225)
XLA Ops:
  67.9 11.9 %collective-permute-done.10 = bf16[256,384]{1,0:T(8,128)(2,1)S(1)} collective-permute-done((bf16[256,384]{1,0:T(8,128)(2,1)}, bf16[256,384]{1,0:T(8,128)(2,1)S(1)}, u32[]{:S(2)}, u32[]{:S(2)}) %collective-permute-start.10) | collective-permute-done | bytes 196640 | tf_op jit(solution)/shard_map/ppermute | solution.py:498
  79.8 4.5 collective-permute-done.11
  98.5 16.3 %collective-permute-done.43 = bf16[128,1024]{1,0:T(8,128)(2,1)S(1)} collective-permute-done((bf16[128,1024]{1,0:T(8,128)(2,1)S(1)}, bf16[128,1024]{1,0:T(8,128)(2,1)S(1)}, u32[]{:S(2)}, u32[]{:S(2)}) %collective-permute-start.43) | collective-permute-done | bytes 262176 | tf_op jit(solution)/shard_map/ppermute | solution.py:358
  129.4 11.7 %collective-permute-done.31 = bf16[32,5120]{1,0:T(8,128)(2,1)S(1)} collective-permute-done((bf16[32,5120]{1,0:T(8,128)(2,1)S(1)}, bf16[32,5120]{1,0:T(8,128)(2,1)S(1)}, u32[]{:S(2)}, u32[]{:S(2)}) %collective-permute-start.31) | collective-permute-done | bytes 327712 | tf_op jit(solution)/shard_map/ppermute | solution.py:355
  146.8 6.6 collective-permute-done.47
  158.7 8.5 %collective-permute-done.44 = bf16[256,1024]{1,0:T(8,128)(2,1)S(1)} collective-permute-done((bf16[256,1024]{1,0:T(8,128)(2,1)S(1)}, bf16[256,1024]{1,0:T(8,128)(2,1)S(1)}, u32[]{:S(2)}, u32[]{:S(2)}) %collective-permute-start.44) | collective-permute-done | bytes 524320 | tf_op jit(solution)/shard_map/ppermute | solution.py:368
  171.1 12.1 %collective-permute-done.17 = bf16[256,1024]{1,0:T(8,128)(2,1)S(1)} collective-permute-done((bf16[256,1024]{1,0:T(8,128)(2,1)S(1)}, bf16[256,1024]{1,0:T(8,128)(2,1)S(1)}, u32[]{:S(2)}, u32[]{:S(2)}) %collective-permute-start.17) | collective-permute-done | bytes 524320 | tf_op jit(solution)/shard_map/ppermute | solution.py:358
  184.2 14.3 %collective-permute-done.18 = bf16[256,1024]{1,0:T(8,128)(2,1)S(1)} collective-permute-done((bf16[256,1024]{1,0:T(8,128)(2,1)S(1)}, bf16[256,1024]{1,0:T(8,128)(2,1)S(1)}, u32[]{:S(2)}, u32[]{:S(2)}) %collective-permute-start.18) | collective-permute-done | bytes 524320 | tf_op jit(solution)/shard_map/ppermute | solution.py:355
  202.4 8.7 %collective-permute-done.48 = bf16[256,1024]{1,0:T(8,128)(2,1)S(1)} collective-permute-done((bf16[256,1024]{1,0:T(8,128)(2,1)S(1)}, bf16[256,1024]{1,0:T(8,128)(2,1)S(1)}, u32[]{:S(2)}, u32[]{:S(2)}) %collective-permute-start.48) | collective-permute-done | bytes 524320 | tf_op jit(solution)/shard_map/ppermute | solution.py:368
  219.8 11.7 %collective-permute-done.33 = bf16[64,5120]{1,0:T(8,128)(2,1)S(1)} collective-permute-done((bf16[64,5120]{1,0:T(8,128)(2,1)S(1)}, bf16[64,5120]{1,0:T(8,128)(2,1)S(1)}, u32[]{:S(2)}, u32[]{:S(2)}) %collective-permute-start.33) | collective-permute-done | bytes 655392 | tf_op jit(solution)/shard_map/ppermute | solution.py:368
  233.0 11.9 %collective-permute-done.19 = bf16[256,1024]{1,0:T(8,128)(2,1)S(1)} collective-permute-done((bf16[256,1024]{1,0:T(8,128)(2,1)S(1)}, bf16[256,1024]{1,0:T(8,128)(2,1)S(1)}, u32[]{:S(2)}, u32[]{:S(2)}) %collective-permute-start.19) | collective-permute-done | bytes 524320 | tf_op jit(solution)/shard_map/ppermute | solution.py:358
  248.1 20.5 %attend_forward.1 = (bf16[8,2,128,128]{3,2,1,0:T(8,128)(2,1)}, f32[2,128,1024]{2,1,0:T(8,128)}, f32[2,2,1024]{2,1,0:T(2,128)}) custom-call(s32[8]{0:T(128)} %add.696.pos_ref, s32[2,4]{1,0:T(2,128)} %and_select_fusion.1.lo_ref, s32[2,1,1024]{2,1,0:T(1,128)} %broadcast_in_dim.6.start_ref, bf16[8,2,128,128]{3,2,1,0:T(8,128)(2,1)} %constant_dynamic-update-slice_fusion.q_ref, ...), custom_call_target="tpu_custom_call" | custom-call | flops 1073741824 | bytes 4194304 | tf_op jit(solution)/shard_map/attend_forward/pallas_call | solution.py:176
  268.6 4.7 all-to-all-start.1
  322.5 6.5 gelu_forward.1
  329.0 6.4 fusion.222
  337.6 7.8 %fusion.224.ga_ref = f32[256,4096]{1,0:T(8,128)} fusion(bf16[256,1024]{1,0:T(8,128)(2,1)S(1)} %get-tuple-element.128, bf16[4096,1024]{1,0:T(8,128)(2,1)} %constant_dynamic-update-slice_fusion.35), kind=kOutput, calls=%fused_computation.504 | convolution fusion | flops 2147483648 | bytes 13107200 | tf_op jit(solution)/shard_map/dot_general | solution.py:25
  352.6 8.5 %gelu_backward.1 = (bf16[256,4096]{1,0:T(8,128)(2,1)}, f32[1,4096]{1,0:T(1,128)}) custom-call(s32[32]{0:T(128)} %copy-done.118, f32[256,4096]{1,0:T(8,128)} %convolution_add_fusion.h_ref, f32[256,4096]{1,0:T(8,128)} %fusion.224.ga_ref), custom_call_target="tpu_custom_call" | custom-call | flops 20971520 | bytes 10485760 | tf_op jit(solution)/shard_map/gelu_backward/pallas_call | solution.py:306
  361.2 6.5 fusion.225
  390.8 6.0 all-to-all-start.2
  432.8 17.6 %attend_backward.1 = (bf16[8,2,128,128]{3,2,1,0:T(8,128)(2,1)}, bf16[8,2,128,128]{3,2,1,0:T(8,128)(2,1)}, bf16[8,2,128,128]{3,2,1,0:T(8,128)(2,1)}) custom-call(s32[8]{0:T(128)} %add.696.pos_ref, s32[2,4]{1,0:T(2,128)} %and_select_fusion.hi_ref, s32[2,1,1024]{2,1,0:T(1,128)} %broadcast_in_dim.6.start_ref, ...), custom_call_target="tpu_custom_call" | custom-call | flops 2684354560 | bytes 5242880 | tf_op jit(solution)/shard_map/attend_backward/pallas_call | solution.py:206
  455.7 6.1 convolution_convert_fusion.8
  461.8 5.7 fusion.223
  512.2 6.9 %collective-permute-done.94 = bf16[256,1024]{1,0:T(8,128)(2,1)} collective-permute-done((bf16[256,1024]{1,0:T(8,128)(2,1)}, bf16[256,1024]{1,0:T(8,128)(2,1)}, u32[]{:S(2)}, u32[]{:S(2)}) %collective-permute-start.94) | collective-permute-done | bytes 524320 | tf_op jit(solution)/shard_map/ppermute | solution.py:385
  523.3 7.1 %collective-permute-done.91 = bf16[256,1024]{1,0:T(8,128)(2,1)} collective-permute-done((bf16[256,1024]{1,0:T(8,128)(2,1)}, bf16[256,1024]{1,0:T(8,128)(2,1)}, u32[]{:S(2)}, u32[]{:S(2)}) %collective-permute-start.91) | collective-permute-done | bytes 524320 | tf_op jit(solution)/shard_map/ppermute | solution.py:385
  534.4 18.3 %collective-permute-done.82 = bf16[64,4096]{1,0:T(8,128)(2,1)S(1)} collective-permute-done((bf16[64,4096]{1,0:T(8,128)(2,1)}, bf16[64,4096]{1,0:T(8,128)(2,1)S(1)}, u32[]{:S(2)}, u32[]{:S(2)}) %collective-permute-start.82) | collective-permute-done | bytes 524320 | tf_op jit(solution)/shard_map/ppermute | solution.py:385
  556.9 7.1 %collective-permute-done.79 = bf16[64,4096]{1,0:T(8,128)(2,1)S(1)} collective-permute-done((bf16[64,4096]{1,0:T(8,128)(2,1)}, bf16[64,4096]{1,0:T(8,128)(2,1)S(1)}, u32[]{:S(2)}, u32[]{:S(2)}) %collective-permute-start.79) | collective-permute-done | bytes 524320 | tf_op jit(solution)/shard_map/ppermute | solution.py:385
  566.9 8.3 %collective-permute-done.76 = bf16[64,4096]{1,0:T(8,128)(2,1)S(1)} collective-permute-done((bf16[64,4096]{1,0:T(8,128)(2,1)S(1)}, bf16[64,4096]{1,0:T(8,128)(2,1)S(1)}, u32[]{:S(2)}, u32[]{:S(2)}) %collective-permute-start.76) | collective-permute-done | bytes 524320 | tf_op jit(solution)/shard_map/ppermute | solution.py:385
  578.9 6.3 collective-permute-done.73
  606.5 4.5 all-to-all-start.4
  644.9 7.9 %collective-permute-done.92 = bf16[128,1024]{1,0:T(8,128)(2,1)S(1)} collective-permute-done((bf16[128,1024]{1,0:T(8,128)(2,1)}, bf16[128,1024]{1,0:T(8,128)(2,1)S(1)}, u32[]{:S(2)}, u32[]{:S(2)}) %collective-permute-start.92) | collective-permute-done | bytes 262176 | tf_op jit(solution)/shard_map/ppermute | solution.py:386
  668.1 7.6 %collective-permute-done.86 = bf16[32,4096]{1,0:T(8,128)(2,1)S(1)} collective-permute-done((bf16[32,4096]{1,0:T(8,128)(2,1)S(1)}, bf16[32,4096]{1,0:T(8,128)(2,1)S(1)}, u32[]{:S(2)}, u32[]{:S(2)}) %collective-permute-start.86) | collective-permute-done | bytes 262176 | tf_op jit(solution)/shard_map/ppermute | solution.py:390
  677.4 6.1 collective-permute-done.56
  (823 shorter events, 388.7 us)
Async XLA Ops:
  17.4 44.1 %all-to-all-start = ((bf16[8,32,384]{2,1,0:T(8,128)(2,1)}), bf16[8,32,384]{2,1,0:T(8,128)(2,1)}, u32[]{:S(2)}, u32[]{:S(2)}) async-start(bf16[8,32,384]{2,1,0:T(8,128)(2,1)} %reshape.844), calls=%async_computation | async-start | bytes 393216 | tf_op jit(solution)/shard_map/all_to_all | solution.py:423
  31.2 31.4 %collective-permute-start.13 = (bf16[256,1024]{1,0:T(8,128)(2,1)S(1)}, bf16[256,1024]{1,0:T(8,128)(2,1)S(1)}, u32[]{:S(2)}, u32[]{:S(2)}) collective-permute-start(bf16[256,1024]{1,0:T(8,128)(2,1)S(1)} %bitcast.171), channel_id=1, source_target_pairs={{0,1},{1,0},{2,3},{3,2},{4,5},{5,4},{6,7},{7,6},{8,9},{9,8},{10,11... | collective-permute-start | bytes 1572872 | tf_op jit(solution)/shard_map/ppermute | solution.py:358
  31.9 32.6 %collective-permute-start.14 = (bf16[256,1024]{1,0:T(8,128)(2,1)S(1)}, bf16[256,1024]{1,0:T(8,128)(2,1)S(1)}, u32[]{:S(2)}, u32[]{:S(2)}) collective-permute-start(bf16[256,1024]{1,0:T(8,128)(2,1)S(1)} %bitcast.172), channel_id=1, source_target_pairs={{0,2},{1,3},{2,4},{3,5},{4,6},{5,7},{6,0},{7,1},{8,10},{9,11},{10,... | collective-permute-start | bytes 1572872 | tf_op jit(solution)/shard_map/ppermute | solution.py:355
  54.6 60.2 %collective-permute-start.36 = (bf16[256,1024]{1,0:T(8,128)(2,1)}, bf16[256,1024]{1,0:T(8,128)(2,1)}, u32[]{:S(2)}, u32[]{:S(2)}) collective-permute-start(bf16[256,1024]{1,0:T(8,128)(2,1)} %pad_maximum_fusion.9), channel_id=1, source_target_pairs={{0,16},{8,24},{16,0},{24,8},{1,17},{9,25},{17,1},{25,9},{2,18},{10... | collective-permute-start | bytes 1572872 | tf_op jit(solution)/shard_map/ppermute | solution.py:368
  58.9 37.5 %collective-permute-start.42 = (bf16[128,1024]{1,0:T(8,128)(2,1)S(1)}, bf16[128,1024]{1,0:T(8,128)(2,1)S(1)}, u32[]{:S(2)}, u32[]{:S(2)}) collective-permute-start(bf16[128,1024]{1,0:T(8,128)(2,1)S(1)} %collective-permute-done.38), channel_id=1, source_target_pairs={{0,2},{1,3},{2,4},{3,5},{4,6},{5,7},{6,0},{7,1},{8,10},{9,11},{10,... | collective-permute-start | bytes 786440 | tf_op jit(solution)/shard_map/ppermute | solution.py:355
  62.6 56.9 %collective-permute-start.21 = (bf16[64,5120]{1,0:T(8,128)(2,1)}, bf16[64,5120]{1,0:T(8,128)(2,1)S(1)}, u32[]{:S(2)}, u32[]{:S(2)}) collective-permute-start(bf16[64,5120]{1,0:T(8,128)(2,1)} %pad_maximum_fusion.5), channel_id=1, source_target_pairs={{0,16},{8,24},{16,0},{24,8},{1,17},{9,25},{17,1},{25,9},{2,18},{10... | collective-permute-start | bytes 1966088 | tf_op jit(solution)/shard_map/ppermute | solution.py:368
  93.7 63.9 %collective-permute-start.40 = (bf16[256,1024]{1,0:T(8,128)(2,1)S(1)}, bf16[256,1024]{1,0:T(8,128)(2,1)S(1)}, u32[]{:S(2)}, u32[]{:S(2)}) collective-permute-start(bf16[256,1024]{1,0:T(8,128)(2,1)S(1)} %pad_maximum_fusion.10), channel_id=1, source_target_pairs={{0,16},{8,24},{16,0},{24,8},{1,17},{9,25},{17,1},{25,9},{2,18},{10... | collective-permute-start | bytes 1572872 | tf_op jit(solution)/shard_map/ppermute | solution.py:368
  96.4 45.9 %collective-permute-start.15 = (bf16[256,1024]{1,0:T(8,128)(2,1)S(1)}, bf16[256,1024]{1,0:T(8,128)(2,1)S(1)}, u32[]{:S(2)}, u32[]{:S(2)}) collective-permute-start(bf16[256,1024]{1,0:T(8,128)(2,1)S(1)} %collective-permute-done.14), channel_id=1, source_target_pairs={{0,1},{1,0},{2,3},{3,2},{4,5},{5,4},{6,7},{7,6},{8,9},{9,8},{10,11... | collective-permute-start | bytes 1572872 | tf_op jit(solution)/shard_map/ppermute | solution.py:358
  114.8 30.2 %collective-permute-start.16 = (bf16[256,1024]{1,0:T(8,128)(2,1)S(1)}, bf16[256,1024]{1,0:T(8,128)(2,1)S(1)}, u32[]{:S(2)}, u32[]{:S(2)}) collective-permute-start(bf16[256,1024]{1,0:T(8,128)(2,1)S(1)} %collective-permute-done.14), channel_id=1, source_target_pairs={{0,2},{1,3},{2,4},{3,5},{4,6},{5,7},{6,0},{7,1},{8,10},{9,11},{10,... | collective-permute-start | bytes 1572872 | tf_op jit(solution)/shard_map/ppermute | solution.py:355
  142.3 73.8 %collective-permute-start.37 = (bf16[512,1024]{1,0:T(8,128)(2,1)S(1)}, bf16[512,1024]{1,0:T(8,128)(2,1)S(1)}, u32[]{:S(2)}, u32[]{:S(2)}) collective-permute-start(bf16[512,1024]{1,0:T(8,128)(2,1)S(1)} %pad_maximum_fusion.1), channel_id=1, source_target_pairs={{0,8},{8,0},{16,24},{24,16},{1,9},{9,1},{17,25},{25,17},{2,10},{10... | collective-permute-start | bytes 3145736 | tf_op jit(solution)/shard_map/ppermute | solution.py:370
  157.7 121.5 %collective-permute-start.22 = (bf16[128,5120]{1,0:T(8,128)(2,1)S(1)}, bf16[128,5120]{1,0:T(8,128)(2,1)}, u32[]{:S(2)}, u32[]{:S(2)}) collective-permute-start(bf16[128,5120]{1,0:T(8,128)(2,1)S(1)} %pad_maximum_fusion), channel_id=1, source_target_pairs={{0,8},{8,0},{16,24},{24,16},{1,9},{9,1},{17,25},{25,17},{2,10},{10... | collective-permute-start | bytes 3932168 | tf_op jit(solution)/shard_map/ppermute | solution.py:370
  167.2 47.2 %collective-permute-start.29 = (bf16[64,5120]{1,0:T(8,128)(2,1)S(1)}, bf16[64,5120]{1,0:T(8,128)(2,1)S(1)}, u32[]{:S(2)}, u32[]{:S(2)}) collective-permute-start(bf16[64,5120]{1,0:T(8,128)(2,1)S(1)} %pad_maximum_fusion.7), channel_id=1, source_target_pairs={{0,16},{8,24},{16,0},{24,8},{1,17},{9,25},{17,1},{25,9},{2,18},{10... | collective-permute-start | bytes 1966088 | tf_op jit(solution)/shard_map/ppermute | solution.py:368
  168.7 104.6 %collective-permute-start.41 = (bf16[512,1024]{1,0:T(8,128)(2,1)}, bf16[512,1024]{1,0:T(8,128)(2,1)}, u32[]{:S(2)}, u32[]{:S(2)}) collective-permute-start(bf16[512,1024]{1,0:T(8,128)(2,1)} %pad_maximum_fusion.2), channel_id=1, source_target_pairs={{0,8},{8,0},{16,24},{24,16},{1,9},{9,1},{17,25},{25,17},{2,10},{10... | collective-permute-start | bytes 3145736 | tf_op jit(solution)/shard_map/ppermute | solution.py:370
  211.1 81.2 %collective-permute-start.26 = (bf16[128,5120]{1,0:T(8,128)(2,1)}, bf16[128,5120]{1,0:T(8,128)(2,1)}, u32[]{:S(2)}, u32[]{:S(2)}) collective-permute-start(bf16[128,5120]{1,0:T(8,128)(2,1)} %constant_dynamic-update-slice_fusion.26), channel_id=1, source_target_pairs={{0,8},{8,0},{16,24},{24,16},{1,9},{9,1},{17,25},{25,17},{2,10},{10... | collective-permute-start | bytes 3932168 | tf_op jit(solution)/shard_map/ppermute | solution.py:370
  216.1 71.5 %collective-permute-start.45 = (bf16[512,1024]{1,0:T(8,128)(2,1)}, bf16[512,1024]{1,0:T(8,128)(2,1)}, u32[]{:S(2)}, u32[]{:S(2)}) collective-permute-start(bf16[512,1024]{1,0:T(8,128)(2,1)} %pad_maximum_fusion.3), channel_id=1, source_target_pairs={{0,8},{8,0},{16,24},{24,16},{1,9},{9,1},{17,25},{25,17},{2,10},{10... | collective-permute-start | bytes 3145736 | tf_op jit(solution)/shard_map/ppermute | solution.py:370
  244.9 51.5 %collective-permute-start.49 = (bf16[512,1024]{1,0:T(8,128)(2,1)}, bf16[512,1024]{1,0:T(8,128)(2,1)}, u32[]{:S(2)}, u32[]{:S(2)}) collective-permute-start(bf16[512,1024]{1,0:T(8,128)(2,1)} %pad_maximum_fusion.4), channel_id=1, source_target_pairs={{0,8},{8,0},{16,24},{24,16},{1,9},{9,1},{17,25},{25,17},{2,10},{10... | collective-permute-start | bytes 3145736 | tf_op jit(solution)/shard_map/ppermute | solution.py:370
  268.6 37.6 %all-to-all-start.1 = ((bf16[8,2,128,128]{3,2,1,0:T(8,128)(2,1)}), bf16[8,2,128,128]{3,2,1,0:T(8,128)(2,1)}, u32[]{:S(2)}, u32[]{:S(2)}) async-start(bf16[8,2,128,128]{3,2,1,0:T(8,128)(2,1)} %get-tuple-element.19), calls=%async_computation.1 | async-start | bytes 1048576 | tf_op jit(solution)/shard_map/all_to_all | solution.py:423
  390.8 42.0 %all-to-all-start.2 = ((bf16[8,256,128]{2,1,0:T(8,128)(2,1)}), bf16[8,256,128]{2,1,0:T(8,128)(2,1)}, u32[]{:S(2)}, u32[]{:S(2)}) async-start(bf16[8,256,128]{2,1,0:T(8,128)(2,1)} %bitcast.176), calls=%async_computation.2 | async-start | bytes 1048576 | tf_op jit(solution)/shard_map/all_to_all | solution.py:423
  430.9 51.1 %collective-permute-start.96 = (bf16[512,1024]{1,0:T(8,128)(2,1)}, bf16[512,1024]{1,0:T(8,128)(2,1)}, u32[]{:S(2)}, u32[]{:S(2)}) collective-permute-start(bf16[512,1024]{1,0:T(8,128)(2,1)} %convolution_convert_fusion.4), channel_id=1, source_target_pairs={{0,8},{8,0},{16,24},{24,16},{1,9},{9,1},{17,25},{25,17},{2,10},{10... | collective-permute-start | bytes 3145736 | tf_op jit(solution)/shard_map/ppermute | solution.py:381
  431.0 53.5 %collective-permute-start.93 = (bf16[512,1024]{1,0:T(8,128)(2,1)}, bf16[512,1024]{1,0:T(8,128)(2,1)}, u32[]{:S(2)}, u32[]{:S(2)}) collective-permute-start(bf16[512,1024]{1,0:T(8,128)(2,1)} %convolution_convert_fusion.5), channel_id=1, source_target_pairs={{0,8},{8,0},{16,24},{24,16},{1,9},{9,1},{17,25},{25,17},{2,10},{10... | collective-permute-start | bytes 3145736 | tf_op jit(solution)/shard_map/ppermute | solution.py:381
  431.5 61.2 %collective-permute-start.90 = (bf16[512,1024]{1,0:T(8,128)(2,1)}, bf16[512,1024]{1,0:T(8,128)(2,1)}, u32[]{:S(2)}, u32[]{:S(2)}) collective-permute-start(bf16[512,1024]{1,0:T(8,128)(2,1)} %convolution_convert_fusion.6), channel_id=1, source_target_pairs={{0,8},{8,0},{16,24},{24,16},{1,9},{9,1},{17,25},{25,17},{2,10},{10... | collective-permute-start | bytes 3145736 | tf_op jit(solution)/shard_map/ppermute | solution.py:381
  431.6 45.4 %collective-permute-start.81 = (bf16[128,4096]{1,0:T(8,128)(2,1)}, bf16[128,4096]{1,0:T(8,128)(2,1)}, u32[]{:S(2)}, u32[]{:S(2)}) collective-permute-start(bf16[128,4096]{1,0:T(8,128)(2,1)} %convolution_convert_fusion), channel_id=1, source_target_pairs={{0,8},{8,0},{16,24},{24,16},{1,9},{9,1},{17,25},{25,17},{2,10},{10... | collective-permute-start | bytes 3145736 | tf_op jit(solution)/shard_map/ppermute | solution.py:381
  432.0 47.3 %collective-permute-start.78 = (bf16[128,4096]{1,0:T(8,128)(2,1)}, bf16[128,4096]{1,0:T(8,128)(2,1)}, u32[]{:S(2)}, u32[]{:S(2)}) collective-permute-start(bf16[128,4096]{1,0:T(8,128)(2,1)} %convolution_convert_fusion.1), channel_id=1, source_target_pairs={{0,8},{8,0},{16,24},{24,16},{1,9},{9,1},{17,25},{25,17},{2,10},{10... | collective-permute-start | bytes 3145736 | tf_op jit(solution)/shard_map/ppermute | solution.py:381
  472.5 33.9 %all-to-all-start.3 = ((bf16[4,256,384]{2,1,0:T(8,128)(2,1)}), bf16[4,256,384]{2,1,0:T(8,128)(2,1)}, u32[]{:S(2)}, u32[]{:S(2)}) async-start(bf16[4,256,384]{2,1,0:T(8,128)(2,1)} %bitcast.180), calls=%async_computation.3 | async-start | bytes 1572864 | tf_op jit(solution)/shard_map/all_to_all | solution.py:423
  489.5 97.8 %collective-permute-start.52 = (bf16[256,1024]{1,0:T(8,128)(2,1)}, bf16[256,1024]{1,0:T(8,128)(2,1)}, u32[]{:S(2)}, u32[]{:S(2)}) collective-permute-start(bf16[256,1024]{1,0:T(8,128)(2,1)} %get-tuple-element.137), channel_id=1, source_target_pairs={{0,1},{1,0},{2,3},{3,2},{4,5},{5,4},{6,7},{7,6},{8,9},{9,8},{10,11... | collective-permute-start | bytes 1572872 | tf_op jit(solution)/shard_map/ppermute | solution.py:397
  490.7 168.3 %collective-permute-start.51 = (bf16[256,1024]{1,0:T(8,128)(2,1)}, bf16[256,1024]{1,0:T(8,128)(2,1)}, u32[]{:S(2)}, u32[]{:S(2)}) collective-permute-start(bf16[256,1024]{1,0:T(8,128)(2,1)} %get-tuple-element.138), channel_id=1, source_target_pairs={{0,1},{1,0},{2,3},{3,2},{4,5},{5,4},{6,7},{7,6},{8,9},{9,8},{10,11... | collective-permute-start | bytes 1572872 | tf_op jit(solution)/shard_map/ppermute | solution.py:397
  508.4 89.6 %collective-permute-start.88 = (bf16[256,1024]{1,0:T(8,128)(2,1)}, bf16[256,1024]{1,0:T(8,128)(2,1)}, u32[]{:S(2)}, u32[]{:S(2)}) collective-permute-start(bf16[256,1024]{1,0:T(8,128)(2,1)} %slice.1039), channel_id=1, source_target_pairs={{16,0},{24,8},{0,16},{8,24},{17,1},{25,9},{1,17},{9,25},{18,2},{26... | collective-permute-start | bytes 1572872 | tf_op jit(solution)/shard_map/ppermute | solution.py:385
  519.1 33.6 %collective-permute-start.82 = (bf16[64,4096]{1,0:T(8,128)(2,1)}, bf16[64,4096]{1,0:T(8,128)(2,1)S(1)}, u32[]{:S(2)}, u32[]{:S(2)}) collective-permute-start(bf16[64,4096]{1,0:T(8,128)(2,1)} %slice.1040), channel_id=1, source_target_pairs={{16,0},{24,8},{0,16},{8,24},{17,1},{25,9},{1,17},{9,25},{18,2},{26... | collective-permute-start | bytes 1572872 | tf_op jit(solution)/shard_map/ppermute | solution.py:385
  530.4 33.6 %collective-permute-start.79 = (bf16[64,4096]{1,0:T(8,128)(2,1)}, bf16[64,4096]{1,0:T(8,128)(2,1)S(1)}, u32[]{:S(2)}, u32[]{:S(2)}) collective-permute-start(bf16[64,4096]{1,0:T(8,128)(2,1)} %slice.1041), channel_id=1, source_target_pairs={{16,0},{24,8},{0,16},{8,24},{17,1},{25,9},{1,17},{9,25},{18,2},{26... | collective-permute-start | bytes 1572872 | tf_op jit(solution)/shard_map/ppermute | solution.py:385
  585.2 30.4 %collective-permute-start.98 = (bf16[128,1024]{1,0:T(8,128)(2,1)}, bf16[128,1024]{1,0:T(8,128)(2,1)}, u32[]{:S(2)}, u32[]{:S(2)}) collective-permute-start(bf16[128,1024]{1,0:T(8,128)(2,1)} %slice.1048), channel_id=1, source_target_pairs={{0,1},{1,0},{2,3},{3,2},{4,5},{5,4},{6,7},{7,6},{8,9},{9,8},{10,11... | collective-permute-start | bytes 786440 | tf_op jit(solution)/shard_map/ppermute | solution.py:386
  587.3 46.5 %collective-permute-start.95 = (bf16[128,1024]{1,0:T(8,128)(2,1)}, bf16[128,1024]{1,0:T(8,128)(2,1)S(1)}, u32[]{:S(2)}, u32[]{:S(2)}) collective-permute-start(bf16[128,1024]{1,0:T(8,128)(2,1)} %slice.1049), channel_id=1, source_target_pairs={{0,1},{1,0},{2,3},{3,2},{4,5},{5,4},{6,7},{7,6},{8,9},{9,8},{10,11... | collective-permute-start | bytes 786440 | tf_op jit(solution)/shard_map/ppermute | solution.py:386
  633.8 43.6 %collective-permute-start.50 = (bf16[256,1024]{1,0:T(8,128)(2,1)}, bf16[256,1024]{1,0:T(8,128)(2,1)S(1)}, u32[]{:S(2)}, u32[]{:S(2)}) collective-permute-start(bf16[256,1024]{1,0:T(8,128)(2,1)} %get-tuple-element.135), channel_id=1, source_target_pairs={{0,1},{1,0},{2,3},{3,2},{4,5},{5,4},{6,7},{7,6},{8,9},{9,8},{10,11... | collective-permute-start | bytes 1572872 | tf_op jit(solution)/shard_map/ppermute | solution.py:397
  (209 other events, 3281.4 us)
